TPU v7x, 128 devices: a whole 4x4x4 slice. The times are simulated.
128 devices in a mesh: row: 16 (over y, z), col: 8 (over x, core).
Axes of the slice: x: 4, y: 4, z: 4, core: 2. Of those that a mesh axis runs over, the one named last changes fastest.
Arguments:
- a_blocks: bfloat16 [16, 4096, 4096], P('col', 'row'), may hold values from -0.19921875 to 0.19921875
- a_row: int32 [16, 4096], P(None, 'row'), may hold values from 0 to 31
- a_col: int32 [16, 4096], P(None, 'row'), may hold values from 0 to 15
- p_blocks: bfloat16 [16, 1024, 4096], P('row', 'col'), may hold values from -6 to 6
- p_row: int32 [16, 1024], P(None, 'col'), may hold values from 0 to 15
- p_col: int32 [16, 1024], P(None, 'col'), may hold values from 0 to 15
- q_blocks: bfloat16 [512, 4096], P('row'), may hold values from -0.75 to 0.75
- sched: int32 [2], replicated, may hold values from 0 to 15, as said below
- fine_agg: int32 [512], replicated, may hold values from 0 to 63, as said below
- coarse_place: int32 [64], replicated, may hold values from 0 to 63, as said below
- prod_cols: int32 [512, 64], P(None, 'col'), may hold values from 0 to 15, as said below
Outputs:
- coarse: float32 [4096, 8192], P('row', 'col')
Inputs may be any that keep to these rules, and one draw needn't show every extreme that they name: `sched`: the 2 panels are distinct, and one of them is the last panel. `fine_agg`: aggregate a belongs to owner coarse_place[a] // 4. Of the 32 fine block rows of one row group (rows i * 32 to i * 32 + 31) at most 10 lie in aggregates of one owner, and in every row group some owner has exactly 10. `coarse_place`: A permutation of the aggregates. `prod_cols`: the 8 entries of row g for column group j (entries j * 8 to j * 8 + 7) are distinct.
All inputs are finite; a program needn't handle non-finite values.
Results may differ from a plain program's by a relative error of at most 0.004.
Values may be sent and summed in bfloat16 or wider, within the bound.
A program may use at most 192 MiB of HBM per device.

v0:
```python
import jax
import jax.numpy as jnp
from jax import lax
from jax.sharding import PartitionSpec as P

B = 64
FR = 32
KB = 16
CB = 16
SECTIONS = 2


def from_root(x, axis, root):
    return lax.dynamic_index_in_dim(lax.all_gather(x, axis), root, 0, keepdims=False)


def from_root_2(value, axis, source):
    kept = jnp.where(lax.axis_index(axis) == source, value, 0).astype(value.dtype)
    return lax.psum(kept, axis)


def dense_panel(blocks, block_rows, block_cols, height, breadth):
    tiles = blocks.reshape(blocks.shape[0], B, B).astype(jnp.float32)
    grid_sum = jnp.zeros((height, breadth, B, B), jnp.float32).at[block_rows, block_cols].add(tiles)
    return grid_sum.transpose(0, 2, 1, 3).reshape(height * B, breadth * B).astype(jnp.bfloat16)


def per_device(
    a_blocks,
    a_row,
    a_col,
    p_blocks,
    p_row,
    p_col,
    q_blocks,
    sched,
    fine_agg,
    coarse_place,
    prod_cols,
):
    panels_held = a_blocks.shape[0]
    groups = lax.axis_size("row")
    own_row = lax.axis_index("row")
    agg_dev = coarse_place.shape[0] // groups
    product = jnp.zeros((FR * B, CB * B), jnp.float32)
    for section in range(SECTIONS):
        panel_id = sched[section]
        mine = lax.dynamic_index_in_dim(a_blocks, panel_id % panels_held, 0, keepdims=False)
        a_values = from_root(mine, "col", panel_id // panels_held)
        p_values = from_root_2(p_blocks[0], "row", panel_id)
        a_dense = dense_panel(a_values, a_row[panel_id], a_col[panel_id], FR, KB)
        p_dense = dense_panel(p_values, p_row[panel_id], p_col[panel_id], KB, CB)
        product = product + jnp.dot(a_dense, p_dense, preferred_element_type=jnp.float32)
    row_start = own_row * FR
    picked_cols = lax.dynamic_slice_in_dim(prod_cols, row_start, FR, 0)
    picked = jnp.take_along_axis(
        product.reshape(FR, B, CB, B), picked_cols[:, None, :, None], axis=2
    )
    restrict = q_blocks.reshape(FR, B, B).astype(jnp.float32)
    contrib = jnp.einsum(
        "rxa,rxqb->raqb", restrict, picked, precision=lax.Precision.HIGHEST
    ).astype(jnp.bfloat16)
    agg_all = coarse_place[fine_agg]
    placing = lax.dynamic_slice_in_dim(agg_all, row_start, FR, 0)
    column_hot = (picked_cols[..., None] == jnp.arange(CB, dtype=jnp.int32)).astype(jnp.bfloat16)
    spread = jnp.einsum(
        "rqc,raqb->racb", column_hot, contrib, preferred_element_type=jnp.float32
    ).astype(jnp.bfloat16)
    target_hot = (
        placing[:, None]
        == jnp.arange(agg_dev * B * lax.axis_size("row") // B, dtype=jnp.int32)[None, :]
    ).astype(jnp.bfloat16)
    term = jnp.einsum("rp,racb->pacb", target_hot, spread, preferred_element_type=jnp.float32)
    return lax.psum_scatter(
        term.reshape(agg_dev * B * lax.axis_size("row"), CB * B),
        "row",
        scatter_dimension=0,
        tiled=True,
    )


def solution(mesh):
    in_specs = (
        P("col", "row", None),
        P(None, "row"),
        P(None, "row"),
        P("row", "col", None),
        P(None, "col"),
        P(None, "col"),
        P("row", None),
        P(),
        P(),
        P(),
        P(None, "col"),
    )
    out_specs = P("row", "col")
    return jax.shard_map(
        per_device, mesh=mesh, in_specs=in_specs, out_specs=out_specs, check_vma=False
    )
```

profile of v0, /device:TPU:6, one launch (start us, length us, event | category | flops | bytes accessed | tf_op | source)
XLA Modules:
  0.0 698.6 jit_solution(12148663951828677082)
XLA Ops:
  7.4 1.3 fusion.35
  9.9 1.6 copy.47
  11.6 1.5 broadcast_select_fusion
  16.9 4.8 constant_dynamic-slice_fusion.3
  29.8 40.0 %select_select_fusion = s32[512]{0:T(512)S(1)} fusion(s32[512]{0:T(512)S(1)} %copy-done.5, s32[]{:T(128)} %bitcast, s32[]{:T(128)} %bitcast.1, s32[]{:T(128)} %bitcast.2, s32[]{:T(128)} %bitcast.3, s32[]{:T(128)} %bitcast.4, s32[]{:T(128)} %bitcast.5, s32[]{:T(128)} %bitcast.6, s32[]{:T(128)} %bitcast.7, s32[]{:T(128)} %bitcast.8, s32[]{:T(128)} %bitcast.9, ...), kind=kLoop, calls=%fused_computation.55 | loop fusion | flops 66048 | bytes 4352 | tf_op jit(solution)/shard_map/gather | solution.py:63
  71.5 0.8 or_select_fusion
  72.2 34.6 %all-reduce.3.cloned.1.call-done = (bf16[128,64,64]{0,2,1:T(8,128)(2,1)}, bf16[128,64,64]{0,2,1:T(8,128)(2,1)}) async-done(((bf16[128,64,64]{0,2,1:T(8,128)(2,1)}, bf16[128,64,64]{0,2,1:T(8,128)(2,1)}), (bf16[128,64,64]{0,2,1:T(8,128)(2,1)}, bf16[128,64,64]{0,2,1:T(8,128)(2,1)})) %all-reduce.3.cloned.1.call-update) | async-done | bytes 2097168 | tf_op jit(solution)/shard_map/psum | solution.py:19
  106.9 4.9 copy.48
  111.8 4.7 copy.54
  116.5 4.5 broadcast.158.clone
  121.0 22.2 %scatter_fusion.1 = f32[16,16,64,64]{3,2,1,0:T(8,128)} fusion(f32[16,16,64,64]{3,2,1,0:T(8,128)} %broadcast.158.clone, s32[128]{0:T(128)S(1)} %get-tuple-element.16, f32[128,64,64]{2,1,0:T(8,128)} %copy.48), kind=kCustom, calls=%fused_computation.2 | custom fusion | flops 524288 | bytes 6292480 | tf_op jit(solution)/shard_map/scatter-add | solution.py:24
  143.2 4.6 convert_bitcast_fusion.5
  147.8 5.7 copy.49
  153.5 6.6 convert_element_type.87
  160.0 4.3 broadcast.158.clone.1
  164.3 21.9 %scatter_fusion.3 = f32[16,16,64,64]{3,2,1,0:T(8,128)} fusion(f32[16,16,64,64]{3,2,1,0:T(8,128)} %broadcast.158.clone.1, s32[128]{0:T(128)S(1)} %get-tuple-element.15, f32[128,64,64]{2,1,0:T(8,128)} %copy.54), kind=kCustom, calls=%fused_computation.4 | custom fusion | flops 524288 | bytes 6292480 | tf_op jit(solution)/shard_map/scatter-add | solution.py:24
  186.2 4.7 convert_bitcast_fusion.4
  190.9 5.7 copy.55
  196.6 6.5 convert_element_type.97
  203.1 3.1 constant_dynamic-slice_fusion.2
  206.2 3.3 copy.67
  209.5 3.1 constant_dynamic-slice_fusion.8
  212.7 4.1 copy.66
  216.7 7.5 %copy.45 = f32[256,64,64]{2,1,0:T(8,128)} copy(bf16[256,64,64]{0,2,1:T(8,128)(2,1)} %bitcast.172) | data formatting | bytes 6291456 | tf_op jit(solution)/shard_map/convert_element_type | solution.py:23
  224.3 6.5 copy.51
  230.8 7.9 %broadcast.154.clone = f32[32,16,64,64]{3,2,1,0:T(8,128)} broadcast(f32[]{:T(128)} %constant.81.clone.1), dimensions={} | broadcast | bytes 8388612 | tf_op jit(solution)/shard_map/broadcast.13
  238.6 41.6 %scatter_fusion = f32[32,16,64,64]{3,2,1,0:T(8,128)} fusion(f32[32,16,64,64]{3,2,1,0:T(8,128)} %broadcast.154.clone, s32[256]{0:T(256)S(1)} %bitcast.170, f32[256,64,64]{2,1,0:T(8,128)} %copy.45), kind=kCustom, calls=%fused_computation.1 | custom fusion | flops 1048576 | bytes 12584960 | tf_op jit(solution)/shard_map/scatter-add | solution.py:24
  280.3 9.8 %convert_bitcast_fusion.2 = bf16[32,64,16,64]{3,1,2,0:T(8,128)(2,1)} fusion(f32[32,16,64,64]{3,2,1,0:T(8,128)} %scatter_fusion), kind=kLoop, calls=%fused_computation.12 | loop fusion | flops 2097152 | bytes 12582912 | tf_op jit(solution)/shard_map/convert_element_type | solution.py:25
  290.1 23.0 %copy.46 = bf16[32,64,16,64]{3,2,1,0:T(8,128)(2,1)} copy(bf16[32,64,16,64]{3,1,2,0:T(8,128)(2,1)} %convert_bitcast_fusion.2) | data formatting | bytes 8388608 | tf_op jit(solution)/shard_map/convert_element_type | solution.py:25
  313.1 11.9 %convert_element_type.82 = bf16[2048,1024]{1,0:T(8,128)(2,1)} reshape(bf16[32,64,16,64]{3,2,1,0:T(8,128)(2,1)} %copy.46) | data formatting | bytes 8388608 | tf_op jit(solution)/shard_map/convert_element_type | solution.py:25
  325.0 7.9 %broadcast.154.clone.1 = f32[32,16,64,64]{3,2,1,0:T(8,128)} broadcast(f32[]{:T(128)} %constant.81.clone.1), dimensions={} | broadcast | bytes 8388612 | tf_op jit(solution)/shard_map/broadcast.13
  332.9 41.6 %scatter_fusion.2 = f32[32,16,64,64]{3,2,1,0:T(8,128)} fusion(f32[32,16,64,64]{3,2,1,0:T(8,128)} %broadcast.154.clone.1, s32[256]{0:T(256)S(1)} %bitcast.169, f32[256,64,64]{2,1,0:T(8,128)} %copy.51), kind=kCustom, calls=%fused_computation.3 | custom fusion | flops 1048576 | bytes 12584960 | tf_op jit(solution)/shard_map/scatter-add | solution.py:24
  374.5 9.8 %convert_bitcast_fusion.1 = bf16[32,64,16,64]{3,1,2,0:T(8,128)(2,1)} fusion(f32[32,16,64,64]{3,2,1,0:T(8,128)} %scatter_fusion.2), kind=kLoop, calls=%fused_computation.11 | loop fusion | flops 2097152 | bytes 12582912 | tf_op jit(solution)/shard_map/convert_element_type | solution.py:25
  384.4 23.0 %copy.52 = bf16[32,64,16,64]{3,2,1,0:T(8,128)(2,1)} copy(bf16[32,64,16,64]{3,1,2,0:T(8,128)(2,1)} %convert_bitcast_fusion.1) | data formatting | bytes 8388608 | tf_op jit(solution)/shard_map/convert_element_type | solution.py:25
  407.4 12.0 %convert_element_type.92 = bf16[2048,1024]{1,0:T(8,128)(2,1)} reshape(bf16[32,64,16,64]{3,2,1,0:T(8,128)(2,1)} %copy.52) | data formatting | bytes 8388608 | tf_op jit(solution)/shard_map/convert_element_type | solution.py:25
  419.4 6.5 fusion.36
  425.9 6.7 convolution_add_fusion
  432.6 13.3 %reshape.283 = f32[32,64,16,64]{3,2,1,0:T(8,128)} reshape(f32[2048,1024]{1,0:T(8,128)} %convolution_add_fusion) | data formatting | bytes 16777216 | tf_op jit(solution)/shard_map/reshape | solution.py:57
  446.0 15.8 %copy.57 = f32[32,64,16,64]{3,1,2,0:T(8,128)} copy(f32[32,64,16,64]{3,2,1,0:T(8,128)} %reshape.283) | data formatting | bytes 16777216 | tf_op jit(solution)/shard_map/reshape | solution.py:57
  461.8 10.2 %gather_fusion = f32[256,64,64]{2,1,0:T(8,128)} fusion(f32[32,64,16,64]{3,1,2,0:T(8,128)} %copy.57, s32[256]{0:T(256)S(1)} %reshape.362), kind=kCustom, calls=%fused_computation | custom fusion | bytes 8390656 | tf_op jit(solution)/shard_map/jit(take_along_axis)/gather | solution.py:56
  471.9 9.0 %copy.58 = f32[32,8,64,64]{2,3,1,0:T(8,128)} copy(f32[32,8,64,64]{3,2,1,0:T(8,128)} %bitcast.168) | data formatting | bytes 8388608 | tf_op jit(solution)/shard_map/jit(take_along_axis)/gather | solution.py:56
  480.9 8.4 %convert_bitcast_fusion.3 = bf16[32,64,8,64]{1,3,2,0:T(8,128)(2,1)} fusion(f32[32,8,64,64]{2,3,1,0:T(8,128)} %copy.58, pred[32,8]{1,0:T(8,128)(4,1)S(1)} %copy.43, bf16[32,64,64,1]{2,1,0,3:T(8,128)(2,1)S(1)} %reshape.398), kind=kOutput, calls=%fused_computation.14 | convolution fusion | flops 807403520 | bytes 6553856 | tf_op jit(solution)/shard_map/rxa,rxqb->raqb/dot_general | solution.py:60
  489.4 7.0 copy.60
  496.3 8.5 %convert_bitcast_fusion = bf16[32,64,16,64]{3,2,1,0:T(8,128)(2,1)} fusion(bf16[32,64,8,64]{3,2,1,0:T(8,128)(2,1)} %copy.60, s32[32,8]{1,0:T(8,128)S(1)} %copy.59), kind=kOutput, calls=%fused_computation.10 | convolution fusion | flops 35655680 | bytes 6292480 | tf_op jit(solution)/shard_map/rqc,raqb->racb/dot_general | solution.py:66
  504.9 20.2 %fusion.2 = f32[64,64,16,64]{3,0,2,1:T(8,128)} fusion(bf16[32,64,16,64]{3,2,1,0:T(8,128)(2,1)} %convert_bitcast_fusion, s32[32]{0:T(128)S(1)} %dynamic_slice.44), kind=kOutput, calls=%fused_computation.7 | convolution fusion | flops 268437504 | bytes 20971648 | tf_op jit(solution)/shard_map/rp,racb->pacb/dot_general | solution.py:73
  525.1 27.5 %copy.62 = f32[64,64,16,64]{3,2,1,0:T(8,128)} copy(f32[64,64,16,64]{3,0,2,1:T(8,128)} %fusion.2) | data formatting | bytes 33554432 | tf_op jit(solution)/shard_map/rp,racb->pacb/dot_general | solution.py:73
  552.6 28.3 %reshape.286 = f32[4096,1024]{1,0:T(8,128)} reshape(f32[64,64,16,64]{3,2,1,0:T(8,128)} %copy.62) | data formatting | bytes 33554432 | tf_op jit(solution)/shard_map/reshape | solution.py:75
  580.9 110.0 %reduce-scatter.2.cloned.1.call-done = f32[256,1024]{1,0:T(8,128)} async-done(((f32[4096,1024]{1,0:T(8,128)}), f32[256,1024]{1,0:T(8,128)}) %reduce-scatter.2.cloned.1.call-update) | async-done | bytes 1048592 | tf_op jit(solution)/shard_map/reduce_scatter | solution.py:74
  (35 shorter events, 6.1 us)
Async XLA Ops:
  7.4 99.5 %all-reduce.3.cloned.1.call-start = ((), (), s32[]{:S(2)}) async-start(), calls=%async_computation.4 | async-start | bytes 4194304 | tf_op jit(solution)/shard_map/psum | solution.py:19
  11.6 15.4 %copy-start.3 = (s32[64]{0:T(128)S(1)}, s32[64]{0:T(128)}, u32[]{:S(2)}) copy-start(s32[64]{0:T(128)} %param.20) | copy-start | bytes 772
  11.6 18.3 %copy-start.5 = (s32[512]{0:T(512)S(1)}, s32[512]{0:T(512)}, u32[]{:S(2)}) copy-start(s32[512]{0:T(512)} %param.19) | copy-start | bytes 6148
  13.0 57.1 %copy-start.4 = (bf16[32,4096]{1,0:T(8,128)(2,1)S(1)}, bf16[32,4096]{1,0:T(8,128)(2,1)}, u32[]{:S(2)}) copy-start(bf16[32,4096]{1,0:T(8,128)(2,1)} %param.17) | copy-start | bytes 786436
  13.1 190.0 %all-gather.5.cloned.1.call-start = ((), (), s32[]{:S(2)}) async-start(), calls=%async_computation.2 | async-start | bytes 18874368 | tf_op jit(solution)/shard_map/all_gather | solution.py:14
  21.7 187.8 %all-gather.3.cloned.1.call-start = ((), (), s32[]{:S(2)}) async-start(), calls=%async_computation.1 | async-start | bytes 18874368 | tf_op jit(solution)/shard_map/all_gather | solution.py:14
  22.3 668.6 %reduce-scatter.2.cloned.1.call-start = ((), (), s32[]{:S(2)}) async-start(), calls=%async_computation.3 | async-start | bytes 17825792 | tf_op jit(solution)/shard_map/reduce_scatter | solution.py:74
  407.4 12.0 %copy-start.1 = (bf16[1024,1024]{1,0:T(8,128)(2,1)S(1)}, bf16[1024,1024]{1,0:T(8,128)(2,1)}, u32[]{:S(2)}) copy-start(bf16[1024,1024]{1,0:T(8,128)(2,1)} %convert_element_type.87) | copy-start | bytes 6291460
  419.4 6.5 copy-start
  419.4 6.5 copy-start.2
Sparse Core Ops, SparseCore 0:
  13.2 93.6 all-reduce.2
  581.0 109.8 reduce-scatter.1
Sparse Core Ops, SparseCore 1:
  21.8 85.5 all-gather.4
  109.0 85.3 all-gather.2
where the time goes:
time: 706 us; the launch traced here: 699 us
  local copies, waits for them, and re-layouts  279 us (40%)
  other arithmetic  200 us (28%)
  waiting for transfers between devices  145 us (21%)
  matrix products  50.3 us (7%)
  between operations  24 us (3%)
    scatter-add x4, other arithmetic, dense_panel(): jnp.zeros((height, breadth, B, B), jnp.float32).at[block_rows, block_cols]  127 us
    reduce_scatter x1, waiting for transfers between devices, per_device(): lax.psum_scatter(term.reshape(agg_dev * B * lax.axis_size('row'), CB * B)...  110 us
    convert_element_type x8, local copies, waits for them, and re-layouts, dense_panel(): grid_sum.transpose(0, 2, 1, 3).reshape(height * B, breadth * B)  94.3 us
    gather x1, other arithmetic, per_device(): agg_all = coarse_place[fine_agg]  40 us
    psum x1, waiting for transfers between devices, from_root_2(): return lax.psum(kept, axis)  34.6 us
    reshape x2, local copies, waits for them, and re-layouts, per_device(): product.reshape(FR, B, CB, B)  29.1 us
    convert_element_type x4, other arithmetic, dense_panel(): grid_sum.transpose(0, 2, 1, 3).reshape(height * B, breadth * B)  28.9 us
    reshape x1, local copies, waits for them, and re-layouts, per_device(): term.reshape(agg_dev * B * lax.axis_size('row'), CB * B)  28.3 us
  transfers between devices with their start and end apart: 4, of which 2 were waited for; matrix products, arithmetic and copies ran while one was open for 22% of the time, Pallas kernels for 0%

commit v1 on v0

v1 whole, which is shorter than its diff:
```python
import jax
import jax.numpy as jnp
from jax import lax
from jax.experimental import pallas as pl
from jax.experimental.pallas import tpu as pltpu
from jax.sharding import PartitionSpec as P

B = 64
FR = 32
KB = 16
CB = 16
SECTIONS = 2
LANES = 128


def from_root(x, axis, root):
    return lax.dynamic_index_in_dim(lax.all_gather(x, axis), root, 0, keepdims=False)


def from_root_2(value, axis, source):
    kept = jnp.where(lax.axis_index(axis) == source, value, 0).astype(value.dtype)
    return lax.psum(kept, axis)


def halves(x, odd):
    lane = lax.broadcasted_iota(jnp.int32, (x.shape[0], LANES), 1)
    is_odd = jnp.broadcast_to(odd, (x.shape[0], LANES)) == 1
    keep = (lane < 64) != is_odd
    evens, odds = [], []
    for part in range(2):
        own = x[:, part * LANES:(part + 1) * LANES].astype(jnp.float32)
        swapped = pltpu.roll(own, 64, 1)
        evens.append(jnp.where(keep, jnp.where(is_odd, swapped, own), 0.0).astype(jnp.bfloat16))
        odds.append(jnp.where(keep, jnp.where(is_odd, own, swapped), 0.0).astype(jnp.bfloat16))
    return jnp.concatenate(evens, axis=1), jnp.concatenate(odds, axis=1)


def one_hot(position, count):
    rows = lax.broadcasted_iota(jnp.int32, (count, position.shape[1]), 0)
    return jnp.where(rows == position, 1.0, 0.0).astype(jnp.bfloat16)


def dot(a, b):
    return jnp.dot(a, b, preferred_element_type=jnp.float32)


def local_kernel(place, a_ref, p_ref, a_pos, a_odd, p_pos, p_odd, q_ref, mask_ref, out_ref, a_dense, p_rows, p_dense, product):
    row_index = lax.broadcasted_iota(jnp.int32, (256, 256), 0)
    col_index = lax.broadcasted_iota(jnp.int32, (256, 256), 1)
    swap = jnp.where(col_index == (row_index % 16) * 16 + row_index // 16, 1.0, 0.0).astype(jnp.bfloat16)

    for s in range(SECTIONS):
        p_hot = one_hot(p_pos[s], 128)

        @pl.loop(0, 16)
        def _(q):
            lanes = pl.ds(pl.multiple_of(q * 256, 256), 256)
            parts = halves(p_ref[s, :, lanes], p_odd[s])
            for h in range(2):
                placed = dot(p_hot, parts[h]).astype(jnp.bfloat16)
                for part in range(2):
                    start = pl.multiple_of((q * 4 + part * 2 + h) * KB, KB)
                    for j in range(CB // 2):
                        p_rows[pl.ds(start, KB), j * LANES:(j + 1) * LANES] = placed[j * KB:(j + 1) * KB, part * LANES:(part + 1) * LANES]

        for group in range(4):
            ordered = dot(swap, p_rows[group * 256:(group + 1) * 256, :]).astype(jnp.bfloat16)
            for k in range(KB):
                start = s * KB * B + k * B + group * 16
                p_dense[start:start + 16, :] = ordered[k * 16:(k + 1) * 16, :]

    for s in range(SECTIONS):
        a_hot = one_hot(a_pos[s], 256)

        @pl.loop(0, 16)
        def _(q):
            lanes = pl.ds(pl.multiple_of(q * 256, 256), 256)
            parts = halves(a_ref[s, :, lanes], a_odd[s])
            for h in range(2):
                placed = dot(a_hot, parts[h]).astype(jnp.bfloat16)
                for part in range(2):
                    start = pl.multiple_of((q * 4 + part * 2 + h) * FR, FR)
                    for k in range(KB // 2):
                        lane = s * KB * B + k * LANES
                        a_dense[pl.ds(start, FR), lane:lane + LANES] = placed[k * FR:(k + 1) * FR, part * LANES:(part + 1) * LANES]

    for n in range(4):

        @pl.loop(0, 4)
        def _(m):
            start = pl.multiple_of(m * 512, 512)
            tile = dot(a_dense[pl.ds(start, 512), :], p_dense[:, n * 256:(n + 1) * 256])
            product[2 * n, pl.ds(start, 512), :] = tile[:, :LANES]
            product[2 * n + 1, pl.ds(start, 512), :] = tile[:, LANES:]

    @pl.loop(0, 64)
    def _(g):
        out_ref[pl.ds(pl.multiple_of(g * B, B), B), :] = jnp.zeros((B, CB * B), jnp.float32)

    @pl.loop(0, FR)
    def _(i):
        restrict = q_ref[i]
        lhs = jnp.concatenate([restrict, restrict], axis=1)
        rows = pl.ds(pl.multiple_of(place[i] * B, B), B)
        for j in range(0, 8, 2):
            tops, bottoms = [], []
            for t in (j, j + 1):
                block = product[t, pl.ds(i, B, stride=FR), :]
                top = block.astype(jnp.bfloat16)
                tops.append(top)
                bottoms.append((block - top.astype(jnp.float32)).astype(jnp.bfloat16))
            rhs = jnp.concatenate([jnp.concatenate(tops, axis=1), jnp.concatenate(bottoms, axis=1)], axis=0)
            term = dot(lhs, rhs).astype(jnp.bfloat16).astype(jnp.float32)
            lanes = slice(j * LANES, (j + 2) * LANES)
            out_ref[rows, lanes] += term * mask_ref[i, :, lanes]


def local_terms(a, p, a_row, a_col, p_row, p_col, q, place, picked_cols):
    a_pos = ((a_col // 2) * FR + a_row)[:, None, :]
    p_pos = ((p_col // 2) * KB + p_row)[:, None, :]
    a_odd = (a_col % 2)[:, :, None]
    p_odd = (p_col % 2)[:, :, None]
    hit = (picked_cols[:, :, None] == jnp.arange(CB, dtype=jnp.int32)).any(axis=1)
    mask = jnp.repeat(hit.astype(jnp.float32), B, axis=1)[:, None, :]
    q_t = q.reshape(FR, B, B).transpose(0, 2, 1)
    vmem = pl.BlockSpec(memory_space=pltpu.VMEM)
    return pl.pallas_call(
        local_kernel,
        out_shape=jax.ShapeDtypeStruct((64 * B, CB * B), jnp.float32),
        in_specs=[pl.BlockSpec(memory_space=pltpu.SMEM)] + [vmem] * 8,
        out_specs=vmem,
        scratch_shapes=[
            pltpu.VMEM((FR * B, SECTIONS * KB * B), jnp.bfloat16),
            pltpu.VMEM((KB * B, CB * B), jnp.bfloat16),
            pltpu.VMEM((SECTIONS * KB * B, CB * B), jnp.bfloat16),
            pltpu.VMEM((8, FR * B, LANES), jnp.float32),
        ],
        compiler_params=pltpu.CompilerParams(vmem_limit_bytes=60 * 1024 * 1024),
    )(place, a, p, a_pos, a_odd, p_pos, p_odd, q_t, mask)


def per_device(a_blocks, a_row, a_col, p_blocks, p_row, p_col, q_blocks, sched, fine_agg, coarse_place, prod_cols):
    panels_held = a_blocks.shape[0]
    own_row = lax.axis_index("row")
    a_parts, p_parts = [], []
    for section in range(SECTIONS):
        panel_id = sched[section]
        mine = lax.dynamic_index_in_dim(a_blocks, panel_id % panels_held, 0, keepdims=False)
        a_parts.append(from_root(mine, "col", panel_id // panels_held))
        p_parts.append(from_root_2(p_blocks[0], "row", panel_id))
    row_start = own_row * FR
    picked_cols = lax.dynamic_slice_in_dim(prod_cols, row_start, FR, 0)
    place = coarse_place[lax.dynamic_slice_in_dim(fine_agg, row_start, FR, 0)]
    term = local_terms(
        jnp.stack(a_parts), jnp.stack(p_parts), a_row[sched], a_col[sched], p_row[sched], p_col[sched], q_blocks, place, picked_cols
    )
    return lax.psum_scatter(term, "row", scatter_dimension=0, tiled=True)


def solution(mesh):
    in_specs = (
        P("col", "row", None),
        P(None, "row"),
        P(None, "row"),
        P("row", "col", None),
        P(None, "col"),
        P(None, "col"),
        P("row", None),
        P(),
        P(),
        P(),
        P(None, "col"),
    )
    return jax.shard_map(per_device, mesh=mesh, in_specs=in_specs, out_specs=P("row", "col"), check_vma=False)
```

time: 706 us -> 377 us (0.53)
  local copies, waits for them, and re-layouts: 279 us -> 16.7 us
  other arithmetic: 200 us -> 11.6 us
  waiting for transfers between devices: 145 us -> 269 us
  Pallas kernels: 0 us -> 57.3 us
  matrix products: 50.3 us -> 0 us
    scatter-add x4 -> x0, other arithmetic: 127 us -> none  [dense_panel(): jnp.zeros((height, breadth, B, B), jnp.float32).at[block_rows, block_cols]]
    convert_element_type x13 -> x1, local copies, waits for them, and re-layouts: 125 us -> 0.07 us  [local_terms(): mask = jnp.repeat(hit.astype(jnp.float32), B, axis=1)[:, None, :]]
    all_gather x2, waiting for transfers between devices: 0.03 us -> 82.9 us  [from_root(): lax.all_gather(x, axis)]
    pallas_call x0 -> x1, Pallas kernels: none -> 57.3 us  [local_terms(): pl.pallas_call(local_kernel, out_shape=jax.ShapeDtypeStruct((64 * B, CB *...]
    reshape x4 -> x2, local copies, waits for them, and re-layouts: 58 us -> 1.57 us  [local_terms(): q_t = q.reshape(FR, B, B).transpose(0, 2, 1)]
    dot_general x5 -> x0, matrix products: 50.3 us -> none  [the longest x1 20.2 us: per_device(): jnp.einsum('rp,racb->pacb', target_hot, spread, preferred_element_type=jn...]
    gather x2, other arithmetic: 40 us -> 0.02 us  [the longest x1 0.01 us: per_device(): a_col[sched]]
    psum x1, waiting for transfers between devices: 34.6 us -> 72.1 us  [from_root_2(): return lax.psum(kept, axis)]
  transfers between devices with their start and end apart: 4 -> 4, of which waited for: 2 -> 3; matrix products, arithmetic and copies ran while one was open for 22% -> 5% of each run, Pallas kernels for 0% -> 0%
where the time goes in v1:
time: 377 us; the launch traced here: 376 us
  waiting for transfers between devices  269 us (71%)
  Pallas kernels  57.3 us (15%)
  between operations  21.7 us (6%)
  local copies, waits for them, and re-layouts  16.7 us (4%)
  other arithmetic  11.6 us (3%)
    reduce_scatter x1, waiting for transfers between devices, per_device(): return lax.psum_scatter(term, 'row', scatter_dimension=0, tiled=True)  113 us
    all_gather x2, waiting for transfers between devices, from_root(): lax.all_gather(x, axis)  82.9 us
    psum x1, waiting for transfers between devices, from_root_2(): return lax.psum(kept, axis)  72.1 us
    pallas_call x1, Pallas kernels, local_terms(): pl.pallas_call(local_kernel, out_shape=jax.ShapeDtypeStruct((64 * B, CB *...  57.3 us
  transfers between devices with their start and end apart: 4, of which 3 were waited for; matrix products, arithmetic and copies ran while one was open for 5% of the time, Pallas kernels for 0%

profile of v1, /device:TPU:6, one launch (start us, length us, event | category | flops | bytes accessed | tf_op | source)
XLA Modules:
  0.0 376.2 jit_solution(18211912411157190938)
XLA Ops:
  7.4 0.0 copy-start
  7.4 0.0 all-reduce.3.cloned.1.call-start
  7.4 1.3 fusion.3
  10.0 2.7 broadcast_select_fusion.1
  12.7 0.0 all-reduce.3.cloned.1.call-update
  12.8 0.0 all-gather.3.cloned.1.call-start
  16.8 4.8 %constant_dynamic-slice_fusion.4 = (bf16[1,256,4096]{2,1,0:T(8,128)(2,1)}, bf16[1,256,4096]{2,1,0:T(8,128)(2,1)}) fusion(bf16[2,256,4096]{2,1,0:T(8,128)(2,1)} %param.11, s32[]{:T(128)S(6)} %select_n.118, s32[]{:T(128)S(6)} %select_n.122), kind=kLoop, calls=%fused_computation.36 | loop fusion | bytes 8388616 | tf_op jit(solution)/shard_map/jit(dynamic_index_in_dim)/dynamic_slice | solution.py:148
  21.6 0.0 all-gather.3.cloned.1.call-update
  21.6 0.0 copy-start.3
  21.6 0.0 all-gather.5.cloned.1.call-start
  21.7 0.0 copy-start.2
  21.7 0.5 all-gather.5.cloned.1.call-update
  22.2 0.0 reduce-scatter.2.cloned.1.call-start
  23.6 0.8 constant_dynamic-slice_fusion
  24.4 0.1 copy.36
  24.5 0.1 broadcast_in_dim.26
  24.6 0.8 broadcast_in_dim_reshape.3.mask_ref
  25.5 0.0 copy-done.7
  25.5 0.0 copy-done
  25.5 0.6 gather_fusion.1
  26.1 0.0 copy-done.4
  26.1 0.6 gather_fusion.2
  26.6 0.0 copy-done.5
  26.6 0.6 gather_fusion.3
  27.2 0.0 copy-done.6
  27.2 0.6 gather_fusion.4
  27.8 0.1 copy.29
  27.9 0.1 copy.32
  28.1 0.0 copy-done.3
  28.1 0.5 reshape.202
  28.6 1.0 copy.35
  29.6 0.8 compare_select_fusion.4
  30.4 0.0 copy-done.2
  30.4 1.3 gather_fusion
  31.7 0.6 reshape_add_fusion.a_pos
  32.3 0.6 multiply_add_fusion.p_pos
  32.9 0.7 add_select_fusion.1.p_odd
  33.6 0.8 add_select_fusion.a_odd
  34.4 72.1 %all-reduce.3.cloned.1.call-done = (bf16[1,128,4096]{2,1,0:T(8,128)(2,1)}, bf16[1,128,4096]{2,1,0:T(8,128)(2,1)}) async-done(((bf16[1,128,4096]{2,1,0:T(8,128)(2,1)}, bf16[1,128,4096]{2,1,0:T(8,128)(2,1)}), (bf16[1,128,4096]{2,1,0:T(8,128)(2,1)}, bf16[1,128,4096]{2,1,0:T(8,128)(2,1)})) %all-reduce.3.cloned.1.call-update) | async-done | bytes 2097168 | tf_op jit(solution)/shard_map/psum | solution.py:22
  106.5 3.0 pad_maximum_fusion.1.p_ref
  109.6 1.7 constant_dynamic-slice_fusion.3
  111.3 82.9 %all-gather.5.cloned.1.call-done = bf16[8,256,4096]{2,1,0:T(8,128)(2,1)} async-done(((bf16[1,256,4096]{2,1,0:T(8,128)(2,1)}), bf16[8,256,4096]{2,1,0:T(8,128)(2,1)}) %all-gather.5.cloned.1.call-update) | async-done | bytes 16777232 | tf_op jit(solution)/shard_map/all_gather | solution.py:17
  194.2 1.7 constant_dynamic-slice_fusion.1
  196.0 2.3 pad_maximum_fusion.a_ref
  198.3 57.3 %shard_map.109 = f32[4096,1024]{1,0:T(8,128)} custom-call(s32[32]{0:T(128)} %gather_fusion, bf16[2,256,4096]{2,1,0:T(8,128)(2,1)} %pad_maximum_fusion.a_ref, bf16[2,128,4096]{2,1,0:T(8,128)(2,1)} %pad_maximum_fusion.1.p_ref, s32[2,1,256]{2,1,0:T(1,128)} %reshape_add_fusion.a_pos, s32[2,256,1]{2,1,0:T(8,128)} %add_select_fusion.a_odd, ...), custom_call_target="tpu_custom_call" | custom-call | tf_op jit(solution)/shard_map/pallas_call | solution.py:127
  255.6 0.0 reduce-scatter.2.cloned.1.call-update
  255.6 0.0 copy-start.1
  255.6 113.2 %reduce-scatter.2.cloned.1.call-done = f32[256,1024]{1,0:T(8,128)} async-done(((f32[4096,1024]{1,0:T(8,128)}), f32[256,1024]{1,0:T(8,128)}) %reduce-scatter.2.cloned.1.call-update) | async-done | bytes 1048592 | tf_op jit(solution)/shard_map/reduce_scatter | solution.py:157
  (11 shorter events, 0.1 us)
Async XLA Ops:
  7.4 18.1 %copy-start = (s32[16,256]{1,0:T(8,128)S(1)}, s32[16,256]{1,0:T(8,128)}, u32[]{:S(2)}) copy-start(s32[16,256]{1,0:T(8,128)} %param.13) | copy-start | bytes 49156
  7.4 99.2 %all-reduce.3.cloned.1.call-start = ((), (), s32[]{:S(2)}) async-start(), calls=%async_computation.4 | async-start | bytes 4194304 | tf_op jit(solution)/shard_map/psum | solution.py:22
  12.8 96.8 %all-gather.3.cloned.1.call-start = ((), (), s32[]{:S(2)}) async-start(), calls=%async_computation.1 | async-start | bytes 18874368 | tf_op jit(solution)/shard_map/all_gather | solution.py:17
  21.6 3.9 %copy-start.7 = (s32[2]{0:T(128)S(1)}, s32[2]{0:T(128)}, u32[]{:S(2)}) copy-start(s32[2]{0:T(128)} %param.18) | copy-start | bytes 28
  21.6 4.5 %copy-start.4 = (s32[16,256]{1,0:T(8,128)S(1)}, s32[16,256]{1,0:T(8,128)}, u32[]{:S(2)}) copy-start(s32[16,256]{1,0:T(8,128)} %param.12) | copy-start | bytes 49156
  21.6 5.1 %copy-start.5 = (s32[16,128]{1,0:T(8,128)S(1)}, s32[16,128]{1,0:T(8,128)}, u32[]{:S(2)}) copy-start(s32[16,128]{1,0:T(8,128)} %param.16) | copy-start | bytes 24580
  21.6 5.6 %copy-start.6 = (s32[16,128]{1,0:T(8,128)S(1)}, s32[16,128]{1,0:T(8,128)}, u32[]{:S(2)}) copy-start(s32[16,128]{1,0:T(8,128)} %param.15) | copy-start | bytes 24580
  21.6 6.5 %copy-start.3 = (bf16[32,4096]{1,0:T(8,128)(2,1)S(1)}, bf16[32,4096]{1,0:T(8,128)(2,1)}, u32[]{:S(2)}) copy-start(bf16[32,4096]{1,0:T(8,128)(2,1)} %param.17) | copy-start | bytes 786436
  21.6 172.6 %all-gather.5.cloned.1.call-start = ((), (), s32[]{:S(2)}) async-start(), calls=%async_computation.2 | async-start | bytes 18874368 | tf_op jit(solution)/shard_map/all_gather | solution.py:17
  21.7 8.7 %copy-start.2 = (s32[64]{0:T(128)S(1)}, s32[64]{0:T(128)}, u32[]{:S(2)}) copy-start(s32[64]{0:T(128)} %param.20) | copy-start | bytes 772
  22.2 346.6 %reduce-scatter.2.cloned.1.call-start = ((), (), s32[]{:S(2)}) async-start(), calls=%async_computation.3 | async-start | bytes 17825792 | tf_op jit(solution)/shard_map/reduce_scatter | solution.py:157
  255.6 113.2 %copy-start.1 = (s32[16,256]{1,0:T(8,128)S(1)}, s32[16,256]{1,0:T(8,128)}, u32[]{:S(2)}) copy-start(s32[16,256]{1,0:T(8,128)} %param.13) | copy-start | bytes 49156
Sparse Core Ops, SparseCore 0:
  12.9 93.6 all-reduce.2
  255.7 113.0 reduce-scatter.1
Sparse Core Ops, SparseCore 1:
  21.7 85.5 all-gather.2
  108.9 85.3 all-gather.4

commit v2 on v1

--- a/solution.py
+++ b/solution.py
@@ -1,3 +1,5 @@
+import functools
+
 import jax
 import jax.numpy as jnp
 from jax import lax
@@ -11,15 +13,331 @@
 CB = 16
 SECTIONS = 2
 LANES = 128
-
-
-def from_root(x, axis, root):
-    return lax.dynamic_index_in_dim(lax.all_gather(x, axis), root, 0, keepdims=False)
-
-
-def from_root_2(value, axis, source):
-    kept = jnp.where(lax.axis_index(axis) == source, value, 0).astype(value.dtype)
-    return lax.psum(kept, axis)
+AGG_DEV = 4
+
+
+MESH = pl.DeviceIdType.MESH
+LAST = 15
+A_GROUPS = 16
+P_GROUPS = 8
+
+
+def remote(src, dst, send_sem, recv_sem, target):
+    return pltpu.make_async_remote_copy(
+        src_ref=src, dst_ref=dst, send_sem=send_sem, recv_sem=recv_sem, device_id=target, device_id_type=MESH
+    )
+
+
+def greet(targets):
+    barrier = pltpu.get_barrier_semaphore()
+    for target in targets:
+        pl.semaphore_signal(barrier, inc=1, device_id=target, device_id_type=MESH)
+    pl.semaphore_wait(barrier, len(targets))
+
+
+def place_of():
+    row, col = lax.axis_index("row"), lax.axis_index("col")
+    return row // 4, row % 4, col // 2, col % 2
+
+
+def device(y, z, x, core):
+    return (y * 4 + z, x * 2 + core)
+
+
+def gather_kernel(panel, a_ref, p_ref, a_out, p_out, a_buf, p_buf, a_recv, p_recv, a_fwd, a_sib, p_trunk, p_branch, load_sem, out_sem):
+    y, z, x, core = place_of()
+    sibling = device(y, z, x, 1 - core)
+    x_next = [device(y, z, (x + 1) % 4, core), device(y, z, (x + 3) % 4, core)]
+    y_next = [device((y + 1) % 4, z, x, core), device((y + 3) % 4, z, x, core)]
+    z_next = [device(y, (z + 1) % 4, x, core), device(y, (z + 3) % 4, x, core)]
+    greet([sibling] + x_next + y_next + z_next)
+    panels = (LAST, panel)
+    for s, k in enumerate(panels):
+        x_root, core_root = (k // 2) // 2, (k // 2) % 2
+
+        @pl.when((x == x_root) & (core == core_root))
+        def _():
+            pltpu.make_async_copy(a_ref.at[k % 2], a_buf.at[s], load_sem.at[0, s]).start()
+
+        @pl.when((y == k // 4) & (z == k % 4))
+        def _():
+            pltpu.make_async_copy(p_ref.at[0], p_buf.at[s], load_sem.at[1, s]).start()
+
+    for s, k in enumerate(panels):
+        x_root, core_root = (k // 2) // 2, (k // 2) % 2
+
+        @pl.when((x == x_root) & (core == core_root))
+        def _():
+            pltpu.make_async_copy(a_ref.at[k % 2], a_buf.at[s], load_sem.at[0, s]).wait()
+
+        @pl.when((y == k // 4) & (z == k % 4))
+        def _():
+            pltpu.make_async_copy(p_ref.at[0], p_buf.at[s], load_sem.at[1, s]).wait()
+
+    def a_stream(s, k, way, t):
+        x_root, core_root = (k // 2) // 2, (k // 2) % 2
+        ahead = (x - x_root + 4) % 4 if way == 0 else (x_root - x + 4) % 4
+        active = core == core_root
+        g = t - ahead - jnp.where(active, 0, 1)
+        block = way * (A_GROUPS // 2) + g
+
+        @pl.when((g >= 0) & (g < A_GROUPS // 2))
+        def _():
+            here = a_buf.at[s, block]
+
+            @pl.when(jnp.logical_not(active & (ahead == 0)))
+            def _():
+                remote(here, here, a_fwd.at[s, way], a_recv.at[s, block], sibling).wait_recv()
+
+            @pl.when(active & (ahead < 3))
+            def _():
+                remote(here, here, a_fwd.at[s, way], a_recv.at[s, block], x_next[way]).start()
+
+            @pl.when(active)
+            def _():
+                remote(here, here, a_sib.at[s, way], a_recv.at[s, block], sibling).start()
+
+            pltpu.make_async_copy(here, a_out.at[s, block], out_sem.at[0]).start()
+
+    def p_stream(s, k, quarter, t):
+        back = quarter % 2
+        if quarter < 2:
+            first, second, trunk, branch = (y, k // 4), (z, k % 4), y_next, z_next
+        else:
+            first, second, trunk, branch = (z, k % 4), (y, k // 4), z_next, y_next
+        e1 = (first[0] - first[1] + 4) % 4 if back == 0 else (first[1] - first[0] + 4) % 4
+        e2 = (second[0] - second[1] + 4) % 4 if back == 0 else (second[1] - second[0] + 4) % 4
+        g = t - e1 - e2
+
+        @pl.when((g >= 0) & (g < 4))
+        def _():
+            block = quarter * 2 + g // 2
+            lanes = pl.ds(pl.multiple_of((g % 2) * 2048, 2048), 2048)
+            here = p_buf.at[s, block, :, lanes]
+            arrival = p_recv.at[s, quarter * 4 + g]
+
+            @pl.when(e1 + e2 > 0)
+            def _():
+                remote(here, here, p_trunk.at[s, quarter], arrival, sibling).wait_recv()
+
+            @pl.when((e2 == 0) & (e1 < 3))
+            def _():
+                remote(here, here, p_trunk.at[s, quarter], arrival, trunk[back]).start()
+
+            @pl.when(e2 < 3)
+            def _():
+                remote(here, here, p_branch.at[s, quarter], arrival, branch[back]).start()
+
+            pltpu.make_async_copy(here, p_out.at[s, block, :, lanes], out_sem.at[1]).start()
+
+    @pl.loop(0, 12)
+    def _(t):
+        for way in range(2):
+            for s, k in enumerate(panels):
+                a_stream(s, k, way, t)
+        for quarter in range(4):
+            for s, k in enumerate(panels):
+                p_stream(s, k, quarter, t)
+
+    for s, k in enumerate(panels):
+        x_root, core_root = (k // 2) // 2, (k // 2) % 2
+        for way in range(2):
+            ahead = (x - x_root + 4) % 4 if way == 0 else (x_root - x + 4) % 4
+            half = a_buf.at[s, pl.ds(way * (A_GROUPS // 2), A_GROUPS // 2)]
+
+            @pl.when((core == core_root) & (ahead < 3))
+            def _():
+                remote(half, half, a_fwd.at[s, way], a_recv.at[s, 0], sibling).wait_send()
+
+            @pl.when(core == core_root)
+            def _():
+                remote(half, half, a_sib.at[s, way], a_recv.at[s, 0], sibling).wait_send()
+
+        for quarter in range(4):
+            back = quarter % 2
+            first, second = ((y, k // 4), (z, k % 4)) if quarter < 2 else ((z, k % 4), (y, k // 4))
+            e1 = (first[0] - first[1] + 4) % 4 if back == 0 else (first[1] - first[0] + 4) % 4
+            e2 = (second[0] - second[1] + 4) % 4 if back == 0 else (second[1] - second[0] + 4) % 4
+            part = p_buf.at[s, pl.ds(quarter * 2, 2)]
+
+            @pl.when((e2 == 0) & (e1 < 3))
+            def _():
+                remote(part, part, p_trunk.at[s, quarter], p_recv.at[s, 0], sibling).wait_send()
+
+            @pl.when(e2 < 3)
+            def _():
+                remote(part, part, p_branch.at[s, quarter], p_recv.at[s, 0], sibling).wait_send()
+
+    pltpu.make_async_copy(a_buf, a_out, out_sem.at[0]).wait()
+    pltpu.make_async_copy(p_buf, p_out, out_sem.at[1]).wait()
+
+
+def gather_panels(panel, a_blocks, p_blocks):
+    anywhere = pl.BlockSpec(memory_space=pl.ANY)
+    a_shape = (SECTIONS, A_GROUPS, 16, B * B)
+    p_shape = (SECTIONS, P_GROUPS, 16, B * B)
+    return pl.pallas_call(
+        functools.partial(gather_kernel, panel),
+        out_shape=(jax.ShapeDtypeStruct(a_shape, jnp.bfloat16), jax.ShapeDtypeStruct(p_shape, jnp.bfloat16)),
+        in_specs=[anywhere] * 2,
+        out_specs=(anywhere, anywhere),
+        scratch_shapes=[
+            pltpu.VMEM(a_shape, jnp.bfloat16),
+            pltpu.VMEM(p_shape, jnp.bfloat16),
+            pltpu.SemaphoreType.DMA((SECTIONS, A_GROUPS)),
+            pltpu.SemaphoreType.DMA((SECTIONS, 16)),
+            pltpu.SemaphoreType.DMA((SECTIONS, 2)),
+            pltpu.SemaphoreType.DMA((SECTIONS, 2)),
+            pltpu.SemaphoreType.DMA((SECTIONS, 4)),
+            pltpu.SemaphoreType.DMA((SECTIONS, 4)),
+            pltpu.SemaphoreType.DMA((2, SECTIONS)),
+            pltpu.SemaphoreType.DMA((2,)),
+        ],
+        compiler_params=pltpu.CompilerParams(collective_id=1 + panel, has_side_effects=True),
+        name=f"gather_{panel}",
+    )(a_blocks.reshape(2, A_GROUPS, 16, B * B), p_blocks.reshape(1, P_GROUPS, 16, B * B))
+
+
+HALF = 512
+PART = AGG_DEV * B
+
+
+def add_rows(total, extra, count):
+    @pl.loop(0, count)
+    def _(i):
+        total[i] = (total[i].astype(jnp.float32) + extra[i].astype(jnp.float32)).astype(jnp.bfloat16)
+
+
+def reduce_kernel(t_ref, o_ref, own, fwd, in_a, in_b, mid, in2_a, in2_b, local_sem, send, recv, send2, recv2):
+    y, z, x, core = place_of()
+    y_next = [device((y + 1) % 4, z, x, core), device((y + 3) % 4, z, x, core)]
+    z_next = [device(y, (z + 1) % 4, x, core), device(y, (z + 3) % 4, x, core)]
+    greet(y_next + z_next)
+    here = ((y, z), (z, y))
+    nexts = ((y_next, z_next), (z_next, y_next))
+
+    started = []
+    for h in range(2):
+        u = here[h][0]
+        for d in range(2):
+            step = (u + 1) % 4 if d == 0 else (u + 3) % 4
+            copy = remote(t_ref.at[h, (u + 2) % 4, pl.ds(2 * d, 2)], in_a.at[h, d], send.at[h, d, 0], recv.at[h, d, 0], nexts[h][0][d])
+            copy.start()
+            started.append(copy)
+    for h in range(2):
+        u = here[h][0]
+        for d in range(2):
+            step = (u + 1) % 4 if d == 0 else (u + 3) % 4
+            other = 2 * (1 - d)
+            copy = remote(t_ref.at[h, step, pl.ds(other, 2)], in_b.at[h, d, pl.ds(other, 2)], send.at[h, d, 1], recv.at[h, d, 1], nexts[h][0][d])
+            copy.start()
+            started.append(copy)
+            pltpu.make_async_copy(t_ref.at[h, step, pl.ds(2 * d, 2)], fwd.at[h, d], local_sem.at[h, d]).start()
+        pltpu.make_async_copy(t_ref.at[h, u], own.at[h], local_sem.at[h, 2]).start()
+
+    for h in range(2):
+        u = here[h][0]
+        for d in range(2):
+            step = (u + 1) % 4 if d == 0 else (u + 3) % 4
+            pltpu.make_async_copy(t_ref.at[h, step, pl.ds(2 * d, 2)], fwd.at[h, d], local_sem.at[h, d]).wait()
+            remote(in_a.at[h, d], in_a.at[h, d], send.at[h, d, 0], recv.at[h, d, 0], nexts[h][0][d]).wait_recv()
+            for part in range(2):
+                add_rows(fwd.at[h, d, part], in_a.at[h, d, part], 4)
+            copy = remote(fwd.at[h, d], in_b.at[h, d, pl.ds(2 * d, 2)], send.at[h, d, 2], recv.at[h, d, 2], nexts[h][0][d])
+            copy.start()
+            started.append(copy)
+
+    def summed(h, part, i):
+        first = own[h, part, i].astype(jnp.float32) + in_b[h, 0, part, i].astype(jnp.float32)
+        return first + in_b[h, 1, part, i].astype(jnp.float32)
+
+    for h in range(2):
+        u, w = here[h]
+        pltpu.make_async_copy(t_ref.at[h, u], own.at[h], local_sem.at[h, 2]).wait()
+        for d in range(2):
+            other = 2 * (1 - d)
+            for part, index in ((other, 1), (2 * d, 2)):
+                block = in_b.at[h, d, pl.ds(part, 2)]
+                remote(block, block, send.at[h, d, index], recv.at[h, d, index], nexts[h][0][d]).wait_recv()
+
+        opposite = (w + 2) % 4
+
+        @pl.loop(0, 4)
+        def _(i):
+            mid[h, 2, i] = summed(h, opposite, i).astype(jnp.bfloat16)
+
+        for d in range(2):
+            copy = remote(mid.at[h, 2, pl.ds(2 * d, 2)], in2_a.at[h, d], send2.at[h, d, 0], recv2.at[h, d, 0], nexts[h][1][d])
+            copy.start()
+            started.append(copy)
+        for d in range(2):
+            step = (w + 1) % 4 if d == 0 else (w + 3) % 4
+            other = 2 * (1 - d)
+
+            @pl.loop(0, 2)
+            def _(i):
+                mid[h, d, other + i] = summed(h, step, other + i).astype(jnp.bfloat16)
+
+            block = pl.ds(other, 2)
+            copy = remote(mid.at[h, d, block], in2_b.at[h, d, block], send2.at[h, d, 1], recv2.at[h, d, 1], nexts[h][1][d])
+            copy.start()
+            started.append(copy)
+
+    for h in range(2):
+        u, w = here[h]
+        for d in range(2):
+            step = (w + 1) % 4 if d == 0 else (w + 3) % 4
+            remote(in2_a.at[h, d], in2_a.at[h, d], send2.at[h, d, 0], recv2.at[h, d, 0], nexts[h][1][d]).wait_recv()
+
+            @pl.loop(0, 2)
+            def _(i):
+                mid[h, d, 2 * d + i] = (summed(h, step, 2 * d + i) + in2_a[h, d, i].astype(jnp.float32)).astype(jnp.bfloat16)
+
+            block = pl.ds(2 * d, 2)
+            copy = remote(mid.at[h, d, block], in2_b.at[h, d, block], send2.at[h, d, 2], recv2.at[h, d, 2], nexts[h][1][d])
+            copy.start()
+            started.append(copy)
+
+    for h in range(2):
+        u, w = here[h]
+        for d in range(2):
+            other = 2 * (1 - d)
+            for part, index in ((other, 1), (2 * d, 2)):
+                block = in2_b.at[h, d, pl.ds(part, 2)]
+                remote(block, block, send2.at[h, d, index], recv2.at[h, d, index], nexts[h][1][d]).wait_recv()
+
+        @pl.loop(0, 4)
+        def _(i):
+            value = summed(h, w, i) + in2_b[h, 0, i].astype(jnp.float32) + in2_b[h, 1, i].astype(jnp.float32)
+            o_ref[pl.ds(pl.multiple_of(i * B, B), B), h * HALF:(h + 1) * HALF] = value
+
+    for copy in started:
+        copy.wait_send()
+
+
+def reduce_terms(term):
+    return pl.pallas_call(
+        reduce_kernel,
+        out_shape=jax.ShapeDtypeStruct((PART, 2 * HALF), jnp.float32),
+        in_specs=[pl.BlockSpec(memory_space=pl.ANY)],
+        out_specs=pl.BlockSpec(memory_space=pltpu.VMEM),
+        scratch_shapes=[
+            pltpu.VMEM((2, 4, 4, B, HALF), jnp.bfloat16),
+            pltpu.VMEM((2, 2, 2, 4, B, HALF), jnp.bfloat16),
+            pltpu.VMEM((2, 2, 2, 4, B, HALF), jnp.bfloat16),
+            pltpu.VMEM((2, 2, 4, 4, B, HALF), jnp.bfloat16),
+            pltpu.VMEM((2, 3, 4, B, HALF), jnp.bfloat16),
+            pltpu.VMEM((2, 2, 2, B, HALF), jnp.bfloat16),
+            pltpu.VMEM((2, 2, 4, B, HALF), jnp.bfloat16),
+            pltpu.SemaphoreType.DMA((2, 3)),
+            pltpu.SemaphoreType.DMA((2, 2, 3)),
+            pltpu.SemaphoreType.DMA((2, 2, 3)),
+            pltpu.SemaphoreType.DMA((2, 2, 3)),
+            pltpu.SemaphoreType.DMA((2, 2, 3)),
+        ],
+        compiler_params=pltpu.CompilerParams(collective_id=0, has_side_effects=True, vmem_limit_bytes=40 * 1024 * 1024),
+        name="reduce_terms",
+    )(term)
 
 
 def halves(x, odd):
@@ -44,7 +362,7 @@
     return jnp.dot(a, b, preferred_element_type=jnp.float32)
 
 
-def local_kernel(place, a_ref, p_ref, a_pos, a_odd, p_pos, p_odd, q_ref, mask_ref, out_ref, a_dense, p_rows, p_dense, product):
+def local_kernel(place, a_ref, p_ref, a_pos, a_odd, p_pos, p_odd, q_ref, mask_ref, out_ref, a_dense, p_rows, p_dense, product, total, staged, out_sem):
     row_index = lax.broadcasted_iota(jnp.int32, (256, 256), 0)
     col_index = lax.broadcasted_iota(jnp.int32, (256, 256), 1)
     swap = jnp.where(col_index == (row_index % 16) * 16 + row_index // 16, 1.0, 0.0).astype(jnp.bfloat16)
@@ -84,35 +402,47 @@
                         lane = s * KB * B + k * LANES
                         a_dense[pl.ds(start, FR), lane:lane + LANES] = placed[k * FR:(k + 1) * FR, part * LANES:(part + 1) * LANES]
 
-    for n in range(4):
-
-        @pl.loop(0, 4)
-        def _(m):
-            start = pl.multiple_of(m * 512, 512)
-            tile = dot(a_dense[pl.ds(start, 512), :], p_dense[:, n * 256:(n + 1) * 256])
-            product[2 * n, pl.ds(start, 512), :] = tile[:, :LANES]
-            product[2 * n + 1, pl.ds(start, 512), :] = tile[:, LANES:]
-
-    @pl.loop(0, 64)
-    def _(g):
-        out_ref[pl.ds(pl.multiple_of(g * B, B), B), :] = jnp.zeros((B, CB * B), jnp.float32)
-
-    @pl.loop(0, FR)
-    def _(i):
-        restrict = q_ref[i]
-        lhs = jnp.concatenate([restrict, restrict], axis=1)
-        rows = pl.ds(pl.multiple_of(place[i] * B, B), B)
-        for j in range(0, 8, 2):
-            tops, bottoms = [], []
-            for t in (j, j + 1):
-                block = product[t, pl.ds(i, B, stride=FR), :]
-                top = block.astype(jnp.bfloat16)
-                tops.append(top)
-                bottoms.append((block - top.astype(jnp.float32)).astype(jnp.bfloat16))
-            rhs = jnp.concatenate([jnp.concatenate(tops, axis=1), jnp.concatenate(bottoms, axis=1)], axis=0)
-            term = dot(lhs, rhs).astype(jnp.bfloat16).astype(jnp.float32)
-            lanes = slice(j * LANES, (j + 2) * LANES)
-            out_ref[rows, lanes] += term * mask_ref[i, :, lanes]
+    for h in range(2):
+        for n in range(2):
+
+            @pl.loop(0, 4)
+            def _(m):
+                start = pl.multiple_of(m * 512, 512)
+                lane = h * HALF + n * 256
+                tile = dot(a_dense[pl.ds(start, 512), :], p_dense[:, lane:lane + 256])
+                product[2 * n, pl.ds(start, 512), :] = tile[:, :LANES]
+                product[2 * n + 1, pl.ds(start, 512), :] = tile[:, LANES:]
+
+        @pl.loop(0, 64)
+        def _(g):
+            total[g] = jnp.zeros((B, HALF), jnp.float32)
+
+        @pl.loop(0, FR)
+        def _(i):
+            restrict = q_ref[i]
+            lhs = jnp.concatenate([restrict, restrict], axis=1)
+            target = place[h, i]
+            for j in range(0, 4, 2):
+                tops, bottoms = [], []
+                for t in (j, j + 1):
+                    block = product[t, pl.ds(i, B, stride=FR), :]
+                    top = block.astype(jnp.bfloat16)
+                    tops.append(top)
+                    bottoms.append((block - top.astype(jnp.float32)).astype(jnp.bfloat16))
+                rhs = jnp.concatenate([jnp.concatenate(tops, axis=1), jnp.concatenate(bottoms, axis=1)], axis=0)
+                term = dot(lhs, rhs).astype(jnp.bfloat16).astype(jnp.float32)
+                lanes = slice(j * LANES, (j + 2) * LANES)
+                masked = term * mask_ref[i, :, h * HALF + j * LANES:h * HALF + (j + 2) * LANES]
+                total[target, :, lanes] += masked
+
+        @pl.loop(0, 64)
+        def _(g):
+            staged[h, g] = total[g].astype(jnp.bfloat16)
+
+        pltpu.make_async_copy(staged.at[h], out_ref.at[h], out_sem.at[h]).start()
+
+    for h in range(2):
+        pltpu.make_async_copy(staged.at[h], out_ref.at[h], out_sem.at[h]).wait()
 
 
 def local_terms(a, p, a_row, a_col, p_row, p_col, q, place, picked_cols):
@@ -126,35 +456,44 @@
     vmem = pl.BlockSpec(memory_space=pltpu.VMEM)
     return pl.pallas_call(
         local_kernel,
-        out_shape=jax.ShapeDtypeStruct((64 * B, CB * B), jnp.float32),
+        out_shape=jax.ShapeDtypeStruct((2, 64, B, HALF), jnp.bfloat16),
         in_specs=[pl.BlockSpec(memory_space=pltpu.SMEM)] + [vmem] * 8,
-        out_specs=vmem,
+        out_specs=pl.BlockSpec(memory_space=pl.ANY),
         scratch_shapes=[
             pltpu.VMEM((FR * B, SECTIONS * KB * B), jnp.bfloat16),
             pltpu.VMEM((KB * B, CB * B), jnp.bfloat16),
             pltpu.VMEM((SECTIONS * KB * B, CB * B), jnp.bfloat16),
-            pltpu.VMEM((8, FR * B, LANES), jnp.float32),
+            pltpu.VMEM((4, FR * B, LANES), jnp.float32),
+            pltpu.VMEM((64, B, HALF), jnp.float32),
+            pltpu.VMEM((2, 64, B, HALF), jnp.bfloat16),
+            pltpu.SemaphoreType.DMA((2,)),
         ],
         compiler_params=pltpu.CompilerParams(vmem_limit_bytes=60 * 1024 * 1024),
     )(place, a, p, a_pos, a_odd, p_pos, p_odd, q_t, mask)
 
 
 def per_device(a_blocks, a_row, a_col, p_blocks, p_row, p_col, q_blocks, sched, fine_agg, coarse_place, prod_cols):
-    panels_held = a_blocks.shape[0]
     own_row = lax.axis_index("row")
-    a_parts, p_parts = [], []
-    for section in range(SECTIONS):
-        panel_id = sched[section]
-        mine = lax.dynamic_index_in_dim(a_blocks, panel_id % panels_held, 0, keepdims=False)
-        a_parts.append(from_root(mine, "col", panel_id // panels_held))
-        p_parts.append(from_root_2(p_blocks[0], "row", panel_id))
+    other = sched[0] + sched[1] - LAST
+    a, p = lax.switch(other, [functools.partial(gather_panels, k) for k in range(LAST)], a_blocks, p_blocks)
+    order = jnp.stack([jnp.int32(LAST), other])
     row_start = own_row * FR
     picked_cols = lax.dynamic_slice_in_dim(prod_cols, row_start, FR, 0)
     place = coarse_place[lax.dynamic_slice_in_dim(fine_agg, row_start, FR, 0)]
+    owner, member = place // AGG_DEV, place % AGG_DEV
+    turned = ((owner % 4) * 4 + owner // 4) * AGG_DEV + member
     term = local_terms(
-        jnp.stack(a_parts), jnp.stack(p_parts), a_row[sched], a_col[sched], p_row[sched], p_col[sched], q_blocks, place, picked_cols
+        a.reshape(SECTIONS, FR * 8, B * B),
+        p.reshape(SECTIONS, KB * 8, B * B),
+        a_row[order],
+        a_col[order],
+        p_row[order],
+        p_col[order],
+        q_blocks,
+        jnp.stack([place, turned]),
+        picked_cols,
     )
-    return lax.psum_scatter(term, "row", scatter_dimension=0, tiled=True)
+    return reduce_terms(term.reshape(2, 4, 4, 4, B, HALF))
 
 
 def solution(mesh):

time: 377 us -> 180 us (0.48)
  waiting for transfers between devices: 269 us -> 0 us
  Pallas kernels: 57.3 us -> 157 us
  between operations: 21.7 us -> 1.31 us
  other arithmetic: 11.6 us -> 4.21 us
    reduce_scatter x1 -> x0, waiting for transfers between devices: 113 us -> none  [per_device(): return lax.psum_scatter(term, 'row', scatter_dimension=0, tiled=True)]
    pallas_call x1 -> x3, Pallas kernels: 57.3 us -> 157 us  [the longest x1 58.7 us: local_terms(): pl.pallas_call(local_kernel, out_shape=jax.ShapeDtypeStruct((2, 64, B, HA...]
    all_gather x2 -> x0, waiting for transfers between devices: 82.9 us -> none  [from_root(): lax.all_gather(x, axis)]
    psum x1 -> x0, waiting for transfers between devices: 72.1 us -> none  [from_root_2(): return lax.psum(kept, axis)]
    dynamic_slice x3 -> x0, local copies, waits for them, and re-layouts: 8.21 us -> none  [the longest x1 4.75 us: per_device(): lax.dynamic_index_in_dim(a_blocks, panel_id % panels_held, 0, keepdims=Fa...]
    another operation x2 -> x1, other arithmetic: 5.37 us -> 0.55 us  [per_device(): jnp.stack([place, turned])]
    unnamed x16 -> x7, local copies, waits for them, and re-layouts: 0.04 us -> 4.36 us
  transfers between devices with their start and end apart: 4 -> 0, of which waited for: 3 -> 0; matrix products, arithmetic and copies ran while one was open for 5% -> 0% of each run, Pallas kernels for 0% -> 0%
where the time goes in v2:
time: 180 us; the launch traced here: 179 us
  Pallas kernels  157 us (87%)
  local copies, waits for them, and re-layouts  15.9 us (9%)
  other arithmetic  4.21 us (2%)
    pallas_call x1, Pallas kernels, local_terms(): pl.pallas_call(local_kernel, out_shape=jax.ShapeDtypeStruct((2, 64, B, HA...  58.7 us
    pallas_call x1, Pallas kernels, reduce_terms(): pl.pallas_call(reduce_kernel, out_shape=jax.ShapeDtypeStruct((PART, 2 * H...  51.4 us
    pallas_call x1, Pallas kernels, gather_panels(): pl.pallas_call(functools.partial(gather_kernel, panel), out_shape=(jax.Sh...  47.3 us
    unnamed x7, local copies, waits for them, and re-layouts  4.36 us

profile of v2, /device:TPU:6, one launch (start us, length us, event | category | flops | bytes accessed | tf_op | source)
XLA Modules:
  0.0 179.0 jit_solution(4567366725247340556)
XLA Ops:
  0.0 0.0 copy-start
  0.0 0.0 copy-start.2
  0.0 0.8 compare_select_fusion.4
  0.9 1.3 fusion.7
  3.4 0.1 fusion.6
  3.5 1.3 gather_fusion.3
  4.7 1.3 gather_fusion.4
  6.0 0.5 multiply_add_fusion.p_pos
  6.5 0.0 copy-done
  6.5 0.6 gather_fusion.1
  7.1 1.3 gather_fusion.2
  8.4 0.6 reshape_add_fusion.a_pos
  9.0 0.8 constant_dynamic-slice_fusion
  9.7 1.4 gather_fusion
  11.1 0.5 pad_add_fusion.place
  11.7 0.1 copy.28
  11.8 0.1 copy.24
  11.9 0.7 add_select_fusion.1.p_odd
  12.6 0.1 broadcast_in_dim.5
  12.8 0.8 broadcast_in_dim_reshape.3.mask_ref
  13.6 0.1 copy.21
  13.7 0.8 add_select_fusion.a_odd
  14.6 1.5 reshape.577
  16.0 1.0 copy.27
  17.1 0.0 copy-done.2
  17.1 47.5 %conditional.1 = (bf16[2,256,4096]{2,1,0:T(8,128)(2,1)}, bf16[2,128,4096]{2,1,0:T(8,128)(2,1)S(1)}) conditional(s32[]{:T(128)} %bitcast.61, (bf16[2,256,4096]{2,1,0:T(8,128)(2,1)}, bf16[1,128,4096]{2,1,0:T(8,128)(2,1)S(1)}) %tuple.112, (bf16[2,256,4096]{2,1,0:T(8,128)(2,1)}, ...), branch_computations={%region_0.0_spmd, %region_1.0_spmd, %region_2.0_spmd, %region_3.0_... | conditional | bytes 16 | solution.py:478
  17.1 47.3 %gather_0.1 = (bf16[2,16,16,4096]{3,2,1,0:T(8,128)(2,1)}, bf16[2,8,16,4096]{3,2,1,0:T(8,128)(2,1)S(1)}) custom-call(bf16[2,16,16,4096]{3,2,1,0:T(8,128)(2,1)} %bitcast.73, bf16[1,8,16,4096]{3,2,1,0:T(8,128)(2,1)S(1)} %bitcast.88), custom_call_target="tpu_custom_call" | custom-call | tf_op jit(solution)/shard_map/cond/branch_0_fun/gather_0/pallas_call | solution.py:179
  64.6 58.7 %shard_map.109 = bf16[2,64,64,512]{3,2,1,0:T(8,128)(2,1)} custom-call(s32[2,32]{1,0:T(2,128)} %pad_add_fusion.place, bf16[2,256,4096]{2,1,0:T(8,128)(2,1)} %get-tuple-element.159.a_ref, bf16[2,128,4096]{2,1,0:T(8,128)(2,1)S(1)} %get-tuple-element.160.p_ref, s32[2,1,256]{2,1,0:T(1,128)} %reshape_add_fusion.a_pos, s32[2,256,1]{2,1,0:T(8,128)} %add_select_fusion.a_odd, ...), custom_call_target="tpu_custom_call" | custom-call | tf_op jit(solution)/shard_map/pallas_call | solution.py:457
  123.3 0.0 copy-start.1
  123.3 3.4 %copy-done.1 = bf16[2,64,64,512]{3,2,1,0:T(8,128)(2,1)S(1)} copy-done((bf16[2,64,64,512]{3,2,1,0:T(8,128)(2,1)S(1)}, bf16[2,64,64,512]{3,2,1,0:T(8,128)(2,1)}, u32[]{:S(2)}) %copy-start.1) | copy-done | bytes 8388632
  126.7 51.4 %reduce_terms.1 = f32[256,1024]{1,0:T(8,128)S(1)} custom-call(bf16[2,4,4,4,64,512]{5,4,3,2,1,0:T(8,128)(2,1)S(1)} %bitcast.72), custom_call_target="tpu_custom_call" | custom-call | tf_op jit(solution)/shard_map/reduce_terms/pallas_call | solution.py:319
  178.1 1.0 copy.60
  (5 shorter events, 0.1 us)
Async XLA Ops:
  0.0 6.5 %copy-start = (s32[16,256]{1,0:T(8,128)S(1)}, s32[16,256]{1,0:T(8,128)}, u32[]{:S(2)}) copy-start(s32[16,256]{1,0:T(8,128)} %param.28) | copy-start | bytes 49156
  0.0 17.1 %copy-start.2 = (bf16[1,128,4096]{2,1,0:T(8,128)(2,1)S(1)}, bf16[1,128,4096]{2,1,0:T(8,128)(2,1)}, u32[]{:S(2)}) copy-start(bf16[1,128,4096]{2,1,0:T(8,128)(2,1)} %param.29) | copy-start | bytes 3145732
  123.3 3.4 %copy-start.1 = (bf16[2,64,64,512]{3,2,1,0:T(8,128)(2,1)S(1)}, bf16[2,64,64,512]{3,2,1,0:T(8,128)(2,1)}, u32[]{:S(2)}) copy-start(bf16[2,64,64,512]{3,2,1,0:T(8,128)(2,1)} %shard_map.109) | copy-start | bytes 25165828

commit v3 on v2

--- a/solution.py
+++ b/solution.py
@@ -20,6 +20,10 @@
 LAST = 15
 A_GROUPS = 16
 P_GROUPS = 8
+A_CUT = 1
+P_CUT = 4
+A_LAG = 2
+P_LAG = 3
 
 
 def remote(src, dst, send_sem, recv_sem, target):
@@ -78,26 +82,29 @@
         x_root, core_root = (k // 2) // 2, (k // 2) % 2
         ahead = (x - x_root + 4) % 4 if way == 0 else (x_root - x + 4) % 4
         active = core == core_root
-        g = t - ahead - jnp.where(active, 0, 1)
-        block = way * (A_GROUPS // 2) + g
-
-        @pl.when((g >= 0) & (g < A_GROUPS // 2))
+        g = t - A_LAG * ahead - jnp.where(active, 0, 1)
+        block = way * (A_GROUPS // 2) + g // A_CUT
+
+        @pl.when((g >= 0) & (g < A_GROUPS // 2 * A_CUT))
         def _():
-            here = a_buf.at[s, block]
+            width = B * B // A_CUT
+            lanes = pl.ds(pl.multiple_of((g % A_CUT) * width, width), width)
+            here = a_buf.at[s, block, :, lanes]
+            arrival = a_recv.at[s, way * (A_GROUPS // 2) * A_CUT + g]
 
             @pl.when(jnp.logical_not(active & (ahead == 0)))
             def _():
-                remote(here, here, a_fwd.at[s, way], a_recv.at[s, block], sibling).wait_recv()
+                remote(here, here, a_fwd.at[s, way], arrival, sibling).wait_recv()
 
             @pl.when(active & (ahead < 3))
             def _():
-                remote(here, here, a_fwd.at[s, way], a_recv.at[s, block], x_next[way]).start()
+                remote(here, here, a_fwd.at[s, way], arrival, x_next[way]).start()
 
             @pl.when(active)
             def _():
-                remote(here, here, a_sib.at[s, way], a_recv.at[s, block], sibling).start()
-
-            pltpu.make_async_copy(here, a_out.at[s, block], out_sem.at[0]).start()
+                remote(here, here, a_sib.at[s, way], arrival, sibling).start()
+
+            pltpu.make_async_copy(here, a_out.at[s, block, :, lanes], out_sem.at[0]).start()
 
     def p_stream(s, k, quarter, t):
         back = quarter % 2
@@ -107,14 +114,15 @@
             first, second, trunk, branch = (z, k % 4), (y, k // 4), z_next, y_next
         e1 = (first[0] - first[1] + 4) % 4 if back == 0 else (first[1] - first[0] + 4) % 4
         e2 = (second[0] - second[1] + 4) % 4 if back == 0 else (second[1] - second[0] + 4) % 4
-        g = t - e1 - e2
-
-        @pl.when((g >= 0) & (g < 4))
+        g = t - P_LAG * (e1 + e2)
+
+        @pl.when((g >= 0) & (g < 2 * P_CUT))
         def _():
-            block = quarter * 2 + g // 2
-            lanes = pl.ds(pl.multiple_of((g % 2) * 2048, 2048), 2048)
+            block = quarter * 2 + g // P_CUT
+            width = B * B // P_CUT
+            lanes = pl.ds(pl.multiple_of((g % P_CUT) * width, width), width)
             here = p_buf.at[s, block, :, lanes]
-            arrival = p_recv.at[s, quarter * 4 + g]
+            arrival = p_recv.at[s, quarter * 2 * P_CUT + g]
 
             @pl.when(e1 + e2 > 0)
             def _():
@@ -130,7 +138,7 @@
 
             pltpu.make_async_copy(here, p_out.at[s, block, :, lanes], out_sem.at[1]).start()
 
-    @pl.loop(0, 12)
+    @pl.loop(0, max(A_GROUPS // 2 * A_CUT + 3 * A_LAG + 1, 2 * P_CUT + 6 * P_LAG))
     def _(t):
         for way in range(2):
             for s, k in enumerate(panels):
@@ -184,8 +192,8 @@
         scratch_shapes=[
             pltpu.VMEM(a_shape, jnp.bfloat16),
             pltpu.VMEM(p_shape, jnp.bfloat16),
-            pltpu.SemaphoreType.DMA((SECTIONS, A_GROUPS)),
-            pltpu.SemaphoreType.DMA((SECTIONS, 16)),
+            pltpu.SemaphoreType.DMA((SECTIONS, A_GROUPS * A_CUT)),
+            pltpu.SemaphoreType.DMA((SECTIONS, P_GROUPS * P_CUT)),
             pltpu.SemaphoreType.DMA((SECTIONS, 2)),
             pltpu.SemaphoreType.DMA((SECTIONS, 2)),
             pltpu.SemaphoreType.DMA((SECTIONS, 4)),
@@ -335,15 +343,12 @@
             pltpu.SemaphoreType.DMA((2, 2, 3)),
             pltpu.SemaphoreType.DMA((2, 2, 3)),
         ],
-        compiler_params=pltpu.CompilerParams(collective_id=0, has_side_effects=True, vmem_limit_bytes=40 * 1024 * 1024),
+        compiler_params=pltpu.CompilerParams(collective_id=0, has_side_effects=True, vmem_limit_bytes=62 * 1024 * 1024),
         name="reduce_terms",
     )(term)
 
 
-def halves(x, odd):
-    lane = lax.broadcasted_iota(jnp.int32, (x.shape[0], LANES), 1)
-    is_odd = jnp.broadcast_to(odd, (x.shape[0], LANES)) == 1
-    keep = (lane < 64) != is_odd
+def halves(x, is_odd, keep):
     evens, odds = [], []
     for part in range(2):
         own = x[:, part * LANES:(part + 1) * LANES].astype(jnp.float32)
@@ -358,49 +363,72 @@
     return jnp.where(rows == position, 1.0, 0.0).astype(jnp.bfloat16)
 
 
+def parity(cols):
+    odd = (cols % 2).astype(jnp.float32)
+    is_odd = jnp.broadcast_to(odd, (LANES, cols.shape[1])).T > 0.5
+    lane = lax.broadcasted_iota(jnp.int32, is_odd.shape, 1)
+    return is_odd, (lane < 64) != is_odd
+
+
 def dot(a, b):
     return jnp.dot(a, b, preferred_element_type=jnp.float32)
 
 
-def local_kernel(place, a_ref, p_ref, a_pos, a_odd, p_pos, p_odd, q_ref, mask_ref, out_ref, a_dense, p_rows, p_dense, product, total, staged, out_sem):
+UN_Q = 2
+UN_I = 4
+
+
+def local_kernel(sched, fine_agg, coarse_place, a_ref, p_ref, a_row, a_col, p_row, p_col, q_ref, cols_ref, out_ref,
+                 a_dense, p_rows, p_dense, product, total, staged, mask, q_rows, out_sem):
+    own_row = lax.axis_index("row")
     row_index = lax.broadcasted_iota(jnp.int32, (256, 256), 0)
     col_index = lax.broadcasted_iota(jnp.int32, (256, 256), 1)
     swap = jnp.where(col_index == (row_index % 16) * 16 + row_index // 16, 1.0, 0.0).astype(jnp.bfloat16)
-
-    for s in range(SECTIONS):
-        p_hot = one_hot(p_pos[s], 128)
-
-        @pl.loop(0, 16)
-        def _(q):
-            lanes = pl.ds(pl.multiple_of(q * 256, 256), 256)
-            parts = halves(p_ref[s, :, lanes], p_odd[s])
+    panels = (LAST, sched[0] + sched[1] - LAST)
+
+    a_hot, a_par, p_hot, p_par = [], [], [], []
+    for k in panels:
+        pick = pl.ds(k, 1)
+        a_hot.append(one_hot((a_col[pick, :] // 2) * FR + a_row[pick, :], 256))
+        p_hot.append(one_hot((p_col[pick, :] // 2) * KB + p_row[pick, :], 128))
+        a_par.append(parity(a_col[pick, :]))
+        p_par.append(parity(p_col[pick, :]))
+
+    block_of = lax.broadcasted_iota(jnp.int32, (FR, CB * B), 1) // B
+    picked = cols_ref[pl.ds(pl.multiple_of(own_row * FR, FR), FR), :]
+    hit = block_of == picked[:, 0:1]
+    for n in range(1, picked.shape[1]):
+        hit = hit | (block_of == picked[:, n:n + 1])
+    mask[...] = jnp.where(hit, 1.0, 0.0)
+    for r in range(FR):
+        q_rows[r * FR:(r + 1) * FR, :] = q_ref[:, r * LANES:(r + 1) * LANES].astype(jnp.float32)
+
+    @pl.loop(0, 16, unroll=UN_Q)
+    def _(q):
+        lanes = pl.ds(pl.multiple_of(q * 256, 256), 256)
+        for s in range(SECTIONS):
+            parts = halves(p_ref[s, :, lanes], *p_par[s])
             for h in range(2):
-                placed = dot(p_hot, parts[h]).astype(jnp.bfloat16)
+                placed = dot(p_hot[s], parts[h]).astype(jnp.bfloat16)
                 for part in range(2):
                     start = pl.multiple_of((q * 4 + part * 2 + h) * KB, KB)
                     for j in range(CB // 2):
-                        p_rows[pl.ds(start, KB), j * LANES:(j + 1) * LANES] = placed[j * KB:(j + 1) * KB, part * LANES:(part + 1) * LANES]
-
+                        p_rows[s, pl.ds(start, KB), j * LANES:(j + 1) * LANES] = placed[j * KB:(j + 1) * KB, part * LANES:(part + 1) * LANES]
+            parts = halves(a_ref[s, :, lanes], *a_par[s])
+            for h in range(2):
+                placed = dot(a_hot[s], parts[h]).astype(jnp.bfloat16)
+                for part in range(2):
+                    start = pl.multiple_of((h * (B // 2) + q * 2 + part) * FR, FR)
+                    for k in range(KB // 2):
+                        lane = s * KB * B + k * LANES
+                        a_dense[pl.ds(start, FR), lane:lane + LANES] = placed[k * FR:(k + 1) * FR, part * LANES:(part + 1) * LANES]
+
+    for s in range(SECTIONS):
         for group in range(4):
-            ordered = dot(swap, p_rows[group * 256:(group + 1) * 256, :]).astype(jnp.bfloat16)
+            ordered = dot(swap, p_rows[s, group * 256:(group + 1) * 256, :]).astype(jnp.bfloat16)
             for k in range(KB):
                 start = s * KB * B + k * B + group * 16
                 p_dense[start:start + 16, :] = ordered[k * 16:(k + 1) * 16, :]
-
-    for s in range(SECTIONS):
-        a_hot = one_hot(a_pos[s], 256)
-
-        @pl.loop(0, 16)
-        def _(q):
-            lanes = pl.ds(pl.multiple_of(q * 256, 256), 256)
-            parts = halves(a_ref[s, :, lanes], a_odd[s])
-            for h in range(2):
-                placed = dot(a_hot, parts[h]).astype(jnp.bfloat16)
-                for part in range(2):
-                    start = pl.multiple_of((q * 4 + part * 2 + h) * FR, FR)
-                    for k in range(KB // 2):
-                        lane = s * KB * B + k * LANES
-                        a_dense[pl.ds(start, FR), lane:lane + LANES] = placed[k * FR:(k + 1) * FR, part * LANES:(part + 1) * LANES]
 
     for h in range(2):
         for n in range(2):
@@ -417,23 +445,33 @@
         def _(g):
             total[g] = jnp.zeros((B, HALF), jnp.float32)
 
-        @pl.loop(0, FR)
-        def _(i):
-            restrict = q_ref[i]
-            lhs = jnp.concatenate([restrict, restrict], axis=1)
-            target = place[h, i]
-            for j in range(0, 4, 2):
-                tops, bottoms = [], []
-                for t in (j, j + 1):
-                    block = product[t, pl.ds(i, B, stride=FR), :]
-                    top = block.astype(jnp.bfloat16)
-                    tops.append(top)
-                    bottoms.append((block - top.astype(jnp.float32)).astype(jnp.bfloat16))
-                rhs = jnp.concatenate([jnp.concatenate(tops, axis=1), jnp.concatenate(bottoms, axis=1)], axis=0)
-                term = dot(lhs, rhs).astype(jnp.bfloat16).astype(jnp.float32)
-                lanes = slice(j * LANES, (j + 2) * LANES)
-                masked = term * mask_ref[i, :, h * HALF + j * LANES:h * HALF + (j + 2) * LANES]
-                total[target, :, lanes] += masked
+        @pl.loop(0, FR, step=UN_I)
+        def _(first):
+            terms = []
+            for u in range(UN_I):
+                i = first + u
+                pair = q_rows[pl.ds(i, B // 2, stride=FR), :]
+                flipped = jnp.concatenate([pair, pltpu.roll(pair, 64, 1)], axis=0)[:, :B]
+                lhs = jnp.concatenate([flipped, flipped], axis=0).astype(jnp.bfloat16)
+                for j in range(0, 4, 2):
+                    tops, bottoms = [], []
+                    for t in (j, j + 1):
+                        block = product[t, pl.ds(i, B, stride=FR), :]
+                        top = block.astype(jnp.bfloat16)
+                        tops.append(top)
+                        bottoms.append((block - top.astype(jnp.float32)).astype(jnp.bfloat16))
+                    rhs = jnp.concatenate([jnp.concatenate(tops, axis=1), jnp.concatenate(bottoms, axis=1)], axis=0)
+                    term = lax.dot_general(lhs, rhs, (((0,), (0,)), ((), ())), preferred_element_type=jnp.float32)
+                    terms.append(term.astype(jnp.bfloat16).astype(jnp.float32))
+            for u in range(UN_I):
+                i = first + u
+                place = coarse_place[fine_agg[own_row * FR + i]]
+                owner, member = place // AGG_DEV, place % AGG_DEV
+                target = place if h == 0 else ((owner % 4) * 4 + owner // 4) * AGG_DEV + member
+                for j in range(0, 4, 2):
+                    lanes = slice(j * LANES, (j + 2) * LANES)
+                    keep = mask[pl.ds(i, 1), h * HALF + j * LANES:h * HALF + (j + 2) * LANES]
+                    total[target, :, lanes] += terms[u * 2 + j // 2] * keep
 
         @pl.loop(0, 64)
         def _(g):
@@ -445,53 +483,45 @@
         pltpu.make_async_copy(staged.at[h], out_ref.at[h], out_sem.at[h]).wait()
 
 
-def local_terms(a, p, a_row, a_col, p_row, p_col, q, place, picked_cols):
-    a_pos = ((a_col // 2) * FR + a_row)[:, None, :]
-    p_pos = ((p_col // 2) * KB + p_row)[:, None, :]
-    a_odd = (a_col % 2)[:, :, None]
-    p_odd = (p_col % 2)[:, :, None]
-    hit = (picked_cols[:, :, None] == jnp.arange(CB, dtype=jnp.int32)).any(axis=1)
-    mask = jnp.repeat(hit.astype(jnp.float32), B, axis=1)[:, None, :]
-    q_t = q.reshape(FR, B, B).transpose(0, 2, 1)
+def local_terms(sched, fine_agg, coarse_place, a, p, a_row, a_col, p_row, p_col, q, prod_cols):
+    smem = pl.BlockSpec(memory_space=pltpu.SMEM)
     vmem = pl.BlockSpec(memory_space=pltpu.VMEM)
     return pl.pallas_call(
         local_kernel,
         out_shape=jax.ShapeDtypeStruct((2, 64, B, HALF), jnp.bfloat16),
-        in_specs=[pl.BlockSpec(memory_space=pltpu.SMEM)] + [vmem] * 8,
+        in_specs=[smem] * 3 + [vmem] * 8,
         out_specs=pl.BlockSpec(memory_space=pl.ANY),
         scratch_shapes=[
             pltpu.VMEM((FR * B, SECTIONS * KB * B), jnp.bfloat16),
-            pltpu.VMEM((KB * B, CB * B), jnp.bfloat16),
+            pltpu.VMEM((SECTIONS, KB * B, CB * B), jnp.bfloat16),
             pltpu.VMEM((SECTIONS * KB * B, CB * B), jnp.bfloat16),
             pltpu.VMEM((4, FR * B, LANES), jnp.float32),
             pltpu.VMEM((64, B, HALF), jnp.float32),
             pltpu.VMEM((2, 64, B, HALF), jnp.bfloat16),
+            pltpu.VMEM((FR, CB * B), jnp.float32),
+            pltpu.VMEM((FR * B // 2, LANES), jnp.float32),
             pltpu.SemaphoreType.DMA((2,)),
         ],
         compiler_params=pltpu.CompilerParams(vmem_limit_bytes=60 * 1024 * 1024),
-    )(place, a, p, a_pos, a_odd, p_pos, p_odd, q_t, mask)
+        name="local_terms",
+    )(sched, fine_agg, coarse_place, a, p, a_row, a_col, p_row, p_col, q, prod_cols)
 
 
 def per_device(a_blocks, a_row, a_col, p_blocks, p_row, p_col, q_blocks, sched, fine_agg, coarse_place, prod_cols):
-    own_row = lax.axis_index("row")
     other = sched[0] + sched[1] - LAST
     a, p = lax.switch(other, [functools.partial(gather_panels, k) for k in range(LAST)], a_blocks, p_blocks)
-    order = jnp.stack([jnp.int32(LAST), other])
-    row_start = own_row * FR
-    picked_cols = lax.dynamic_slice_in_dim(prod_cols, row_start, FR, 0)
-    place = coarse_place[lax.dynamic_slice_in_dim(fine_agg, row_start, FR, 0)]
-    owner, member = place // AGG_DEV, place % AGG_DEV
-    turned = ((owner % 4) * 4 + owner // 4) * AGG_DEV + member
     term = local_terms(
+        sched,
+        fine_agg,
+        coarse_place,
         a.reshape(SECTIONS, FR * 8, B * B),
         p.reshape(SECTIONS, KB * 8, B * B),
-        a_row[order],
-        a_col[order],
-        p_row[order],
-        p_col[order],
+        a_row,
+        a_col,
+        p_row,
+        p_col,
         q_blocks,
-        jnp.stack([place, turned]),
-        picked_cols,
+        prod_cols,
     )
     return reduce_terms(term.reshape(2, 4, 4, 4, B, HALF))
 

time: 180 us -> 149 us (0.83)
  Pallas kernels: 157 us -> 143 us
  local copies, waits for them, and re-layouts: 15.9 us -> 5.17 us
  other arithmetic: 4.21 us -> 0 us
    pallas_call x1, Pallas kernels: 58.7 us -> 39.3 us  [local_terms(): pl.pallas_call(local_kernel, out_shape=jax.ShapeDtypeStruct((2, 64, B, HA...]
    pallas_call x1, Pallas kernels: 47.3 us -> 53.6 us  [gather_panels(): pl.pallas_call(functools.partial(gather_kernel, panel), out_shape=(jax.Sh...]
    gather x7 -> x0, local copies, waits for them, and re-layouts: 5.97 us -> none  [the longest x2 1.39 us: per_device(): p_col[order]]
    reshape x2 -> x0, local copies, waits for them, and re-layouts: 2.48 us -> none  [local_terms(): q_t = q.reshape(FR, B, B).transpose(0, 2, 1)]
    select_n x4 -> x0, other arithmetic: 2.46 us -> none  [the longest x1 0.84 us: per_device(): place = coarse_place[lax.dynamic_slice_in_dim(fine_agg, row_start, FR, 0)]]
    unnamed x7 -> x2, local copies, waits for them, and re-layouts: 4.36 us -> 3.86 us
where the time goes in v3:
time: 149 us; the launch traced here: 150 us
  Pallas kernels  143 us (96%)
  local copies, waits for them, and re-layouts  5.17 us (3%)
    pallas_call x1, Pallas kernels, gather_panels(): pl.pallas_call(functools.partial(gather_kernel, panel), out_shape=(jax.Sh...  53.6 us
    pallas_call x1, Pallas kernels, reduce_terms(): pl.pallas_call(reduce_kernel, out_shape=jax.ShapeDtypeStruct((PART, 2 * H...  50.2 us
    pallas_call x1, Pallas kernels, local_terms(): pl.pallas_call(local_kernel, out_shape=jax.ShapeDtypeStruct((2, 64, B, HA...  39.3 us
    unnamed x2, local copies, waits for them, and re-layouts  3.86 us

profile of v3, /device:TPU:6, one launch (start us, length us, event | category | flops | bytes accessed | tf_op | source)
XLA Modules:
  0.0 149.8 jit_solution(15033437321124308969)
XLA Ops:
  0.0 1.3 fusion
  2.5 1.6 %copy.12.cols_ref = s32[512,8]{1,0:T(8,128)} copy(s32[512,8]{0,1:T(8,128)} %param.36) | data formatting | bytes 32768 | tf_op args[10]
  4.1 53.8 %conditional.1 = (bf16[2,256,4096]{2,1,0:T(8,128)(2,1)}, bf16[2,128,4096]{2,1,0:T(8,128)(2,1)S(1)}) conditional(s32[]{:T(128)} %bitcast.60, (bf16[2,256,4096]{2,1,0:T(8,128)(2,1)}, bf16[1,128,4096]{2,1,0:T(8,128)(2,1)}) %tuple.95, (bf16[2,256,4096]{2,1,0:T(8,128)(2,1)}, bf16[1,128,4096]{2,1,0:T(8,128)(2,1)}) %tuple.95, ...), branch_computations={%region_0.0_spmd, %region_1.0_spmd, %region_2.0_spmd, %region_3.0_... | conditional | bytes 16 | solution.py:512
  4.1 53.6 %gather_8.1 = (bf16[2,16,16,4096]{3,2,1,0:T(8,128)(2,1)}, bf16[2,8,16,4096]{3,2,1,0:T(8,128)(2,1)S(1)}) custom-call(bf16[2,16,16,4096]{3,2,1,0:T(8,128)(2,1)} %bitcast.70, bf16[1,8,16,4096]{3,2,1,0:T(8,128)(2,1)} %bitcast.85), custom_call_target="tpu_custom_call" | custom-call | tf_op jit(solution)/shard_map/cond/branch_8_fun/gather_8/pallas_call | solution.py:187
  57.9 39.3 %local_terms.1 = bf16[2,64,64,512]{3,2,1,0:T(8,128)(2,1)} custom-call(s32[2]{0:T(128)} %sched.1, s32[512]{0:T(512)} %fine_agg.1, s32[64]{0:T(128)} %coarse_place.1, bf16[2,256,4096]{2,1,0:T(8,128)(2,1)} %get-tuple-element.159.a_ref, bf16[2,128,4096]{2,1,0:T(8,128)(2,1)S(1)} %get-tuple-element.160.p_ref, s32[16,256]{1,0:T(8,128)} %a_row.1, s32[16,256]{1,0:T(8,128)} %a_col.1, ...), custom_call_target="tpu_custom_call" | custom-call | tf_op jit(solution)/shard_map/local_terms/pallas_call | solution.py:489
  97.3 50.2 %reduce_terms.1 = f32[256,1024]{1,0:T(8,128)} custom-call(bf16[2,4,4,4,64,512]{5,4,3,2,1,0:T(8,128)(2,1)} %bitcast.92), custom_call_target="tpu_custom_call" | custom-call | tf_op jit(solution)/shard_map/reduce_terms/pallas_call | solution.py:327
  147.5 2.3 %copy.44 = f32[256,1024]{1,0:T(8,128)} copy(f32[256,1024]{1,0:T(8,128)} %reduce_terms.1) | data formatting | bytes 2097152

commit v4 on v3

--- a/solution.py
+++ b/solution.py
@@ -21,9 +21,8 @@
 A_GROUPS = 16
 P_GROUPS = 8
 A_CUT = 1
-P_CUT = 4
 A_LAG = 2
-P_LAG = 3
+P_TIMES = (5, 7, 8, 10, 13)
 
 
 def remote(src, dst, send_sem, recv_sem, target):
@@ -32,11 +31,12 @@
     )
 
 
-def greet(targets):
+def greet(targets, distant=()):
     barrier = pltpu.get_barrier_semaphore()
-    for target in targets:
+    everyone = list(distant) + list(targets)
+    for target in everyone:
         pl.semaphore_signal(barrier, inc=1, device_id=target, device_id_type=MESH)
-    pl.semaphore_wait(barrier, len(targets))
+    pl.semaphore_wait(barrier, len(everyone))
 
 
 def place_of():
@@ -48,18 +48,20 @@
     return (y * 4 + z, x * 2 + core)
 
 
-def gather_kernel(panel, a_ref, p_ref, a_out, p_out, a_buf, p_buf, a_recv, p_recv, a_fwd, a_sib, p_trunk, p_branch, load_sem, out_sem):
+def gather_kernel(panel, a_ref, p_ref, a_out, p_out, a_buf, p_buf, a_recv, a_fwd, a_sib, line_send, line_recv, across_send, across_recv,
+                  far_send, far_recv, along_send, along_recv, relay_send, relay_recv, load_sem, out_sem):
     y, z, x, core = place_of()
     sibling = device(y, z, x, 1 - core)
     x_next = [device(y, z, (x + 1) % 4, core), device(y, z, (x + 3) % 4, core)]
     y_next = [device((y + 1) % 4, z, x, core), device((y + 3) % 4, z, x, core)]
     z_next = [device(y, (z + 1) % 4, x, core), device(y, (z + 3) % 4, x, core)]
-    greet([sibling] + x_next + y_next + z_next)
     panels = (LAST, panel)
+    chunks = A_GROUPS // 2 * A_CUT
+    width = B * B // A_CUT
+    parts = [pl.ds(0, B * B // 2), pl.ds(B * B // 2, B * B // 2)]
+
     for s, k in enumerate(panels):
-        x_root, core_root = (k // 2) // 2, (k // 2) % 2
-
-        @pl.when((x == x_root) & (core == core_root))
+        @pl.when((x == (k // 2) // 2) & (core == (k // 2) % 2))
         def _():
             pltpu.make_async_copy(a_ref.at[k % 2], a_buf.at[s], load_sem.at[0, s]).start()
 
@@ -67,114 +69,199 @@
         def _():
             pltpu.make_async_copy(p_ref.at[0], p_buf.at[s], load_sem.at[1, s]).start()
 
+    greet([sibling] + x_next + y_next + z_next, [device((y + 2) % 4, z, x, core), device(y, (z + 2) % 4, x, core)])
+
     for s, k in enumerate(panels):
-        x_root, core_root = (k // 2) // 2, (k // 2) % 2
-
-        @pl.when((x == x_root) & (core == core_root))
+        @pl.when((y == k // 4) & (z == k % 4))
+        def _():
+            pltpu.make_async_copy(p_ref.at[0], p_buf.at[s], load_sem.at[1, s]).wait()
+
+        @pl.when((x == (k // 2) // 2) & (core == (k // 2) % 2))
         def _():
             pltpu.make_async_copy(a_ref.at[k % 2], a_buf.at[s], load_sem.at[0, s]).wait()
 
-        @pl.when((y == k // 4) & (z == k % 4))
-        def _():
-            pltpu.make_async_copy(p_ref.at[0], p_buf.at[s], load_sem.at[1, s]).wait()
-
-    def a_stream(s, k, way, t):
+    def a_role(k, way):
         x_root, core_root = (k // 2) // 2, (k // 2) % 2
         ahead = (x - x_root + 4) % 4 if way == 0 else (x_root - x + 4) % 4
-        active = core == core_root
-        g = t - A_LAG * ahead - jnp.where(active, 0, 1)
-        block = way * (A_GROUPS // 2) + g // A_CUT
-
-        @pl.when((g >= 0) & (g < A_GROUPS // 2 * A_CUT))
-        def _():
-            width = B * B // A_CUT
+        active = core == way
+        origin = (ahead == 0) & (core == core_root)
+        onward = active & (ahead < 3)
+        if core_root == way:
+            return ahead, origin, onward, active, A_LAG * ahead + jnp.where(active, 0, 1)
+        lag = jnp.where(origin, 0, A_LAG * ahead + jnp.where(active, 1, 2))
+        return ahead, origin, onward, (active & (ahead > 0)) | origin, lag
+
+    def a_stream(s, k, way, t):
+        ahead, origin, onward, sideways, lag = a_role(k, way)
+        g = t - lag
+
+        @pl.when((g >= 0) & (g < chunks))
+        def _():
+            block = way * (A_GROUPS // 2) + g // A_CUT
             lanes = pl.ds(pl.multiple_of((g % A_CUT) * width, width), width)
             here = a_buf.at[s, block, :, lanes]
-            arrival = a_recv.at[s, way * (A_GROUPS // 2) * A_CUT + g]
-
-            @pl.when(jnp.logical_not(active & (ahead == 0)))
+            arrival = a_recv.at[s, way * chunks + g]
+
+            @pl.when(jnp.logical_not(origin))
             def _():
                 remote(here, here, a_fwd.at[s, way], arrival, sibling).wait_recv()
 
-            @pl.when(active & (ahead < 3))
+            @pl.when(onward)
             def _():
                 remote(here, here, a_fwd.at[s, way], arrival, x_next[way]).start()
 
-            @pl.when(active)
+            @pl.when(sideways)
             def _():
                 remote(here, here, a_sib.at[s, way], arrival, sibling).start()
 
             pltpu.make_async_copy(here, a_out.at[s, block, :, lanes], out_sem.at[0]).start()
 
-    def p_stream(s, k, quarter, t):
-        back = quarter % 2
-        if quarter < 2:
-            first, second, trunk, branch = (y, k // 4), (z, k % 4), y_next, z_next
+    def p_role(k, f):
+        if f == 0:
+            u, w, u_root, w_root, u_next, w_next = y, z, k // 4, k % 4, y_next, z_next
         else:
-            first, second, trunk, branch = (z, k % 4), (y, k // 4), z_next, y_next
-        e1 = (first[0] - first[1] + 4) % 4 if back == 0 else (first[1] - first[0] + 4) % 4
-        e2 = (second[0] - second[1] + 4) % 4 if back == 0 else (second[1] - second[0] + 4) % 4
-        g = t - P_LAG * (e1 + e2)
-
-        @pl.when((g >= 0) & (g < 2 * P_CUT))
-        def _():
-            block = quarter * 2 + g // P_CUT
-            width = B * B // P_CUT
-            lanes = pl.ds(pl.multiple_of((g % P_CUT) * width, width), width)
-            here = p_buf.at[s, block, :, lanes]
-            arrival = p_recv.at[s, quarter * 2 * P_CUT + g]
-
-            @pl.when(e1 + e2 > 0)
-            def _():
-                remote(here, here, p_trunk.at[s, quarter], arrival, sibling).wait_recv()
-
-            @pl.when((e2 == 0) & (e1 < 3))
-            def _():
-                remote(here, here, p_trunk.at[s, quarter], arrival, trunk[back]).start()
-
-            @pl.when(e2 < 3)
-            def _():
-                remote(here, here, p_branch.at[s, quarter], arrival, branch[back]).start()
-
-            pltpu.make_async_copy(here, p_out.at[s, block, :, lanes], out_sem.at[1]).start()
-
-    @pl.loop(0, max(A_GROUPS // 2 * A_CUT + 3 * A_LAG + 1, 2 * P_CUT + 6 * P_LAG))
+            u, w, u_root, w_root, u_next, w_next = z, y, k % 4, k // 4, z_next, y_next
+        du, dw = (u - u_root + 4) % 4, (w - w_root + 4) % 4
+        clear = [jnp.logical_not((dw == 0) & (du == 3)), jnp.logical_not((dw == 0) & (du == 1))]
+        return u, u_root, w_root, u_next, w_next, du, dw, clear
+
+    pairs = [(s, k, f) for s, k in enumerate(panels) for f in range(2)]
+
+    def along(s, f, u, u_next, clear):
+        group = p_buf.at[s, f * 4 + u]
+        for d in range(2):
+            @pl.when(clear[d])
+            def _():
+                remote(group, group, along_send.at[s, f, d], along_recv.at[s, f, d], u_next[d]).start()
+
+    def relay(s, f, u, u_next, clear, d):
+        group = p_buf.at[s, f * 4 + (u + (3 if d == 0 else 1)) % 4, :, parts[d]]
+
+        @pl.when(clear[d])
+        def _():
+            remote(group, group, relay_send.at[s, f, d], relay_recv.at[s, f, d], u_next[d]).start()
+
+    def across(s, f, u, w_next):
+        group = p_buf.at[s, f * 4 + u]
+        for d in range(2):
+            remote(group, group, across_send.at[s, f, d], across_recv.at[s, f, d], w_next[d]).start()
+
+    for s, k, f in pairs:
+        u, u_root, w_root, u_next, w_next, du, dw, clear = p_role(k, f)
+
+        @pl.when((du == 0) & (dw == 0))
+        def _():
+            for j in (2, 1, 3):
+                g = (u_root + j) % 4
+                group = p_buf.at[s, f * 4 + g]
+                target = device(g, w_root, x, core) if f == 0 else device(w_root, g, x, core)
+                remote(group, group, line_send.at[s, f, j - 1], line_recv.at[s, f], target).start()
+            across(s, f, u, w_next)
+            along(s, f, u, u_next, clear)
+            for d in range(2):
+                relay(s, f, u, u_next, clear, d)
+
+    def first_arrivals():
+        for s, k, f in pairs:
+            u, u_root, w_root, u_next, w_next, du, dw, clear = p_role(k, f)
+
+            @pl.when((du != 0) & (dw == 0))
+            def _():
+                group = p_buf.at[s, f * 4 + u]
+                remote(group, group, line_send.at[s, f, 0], line_recv.at[s, f], sibling).wait_recv()
+                across(s, f, u, w_next)
+                along(s, f, u, u_next, clear)
+
+    def second_arrivals():
+        for s, k, f in pairs:
+            u, u_root, w_root, u_next, w_next, du, dw, clear = p_role(k, f)
+            for d in range(2):
+                @pl.when(dw == (1 if d == 0 else 3))
+                def _():
+                    group = p_buf.at[s, f * 4 + u]
+                    remote(group, group, across_send.at[s, f, d], across_recv.at[s, f, d], sibling).wait_recv()
+                    half = p_buf.at[s, f * 4 + u, :, parts[d]]
+                    remote(half, half, far_send.at[s, f, d], far_recv.at[s, f, d], w_next[d]).start()
+                    along(s, f, u, u_next, clear)
+
+    def third_arrivals():
+        for s, k, f in pairs:
+            u, u_root, w_root, u_next, w_next, du, dw, clear = p_role(k, f)
+
+            @pl.when(dw == 2)
+            def _():
+                for d in range(2):
+                    half = p_buf.at[s, f * 4 + u, :, parts[d]]
+                    remote(half, half, far_send.at[s, f, d], far_recv.at[s, f, d], sibling).wait_recv()
+                along(s, f, u, u_next, clear)
+
+    def fourth_arrivals():
+        for s, k, f in pairs:
+            u, u_root, w_root, u_next, w_next, du, dw, clear = p_role(k, f)
+
+            @pl.when((du != 0) | (dw != 0))
+            def _():
+                for d in range(2):
+                    group = p_buf.at[s, f * 4 + (u + (3 if d == 0 else 1)) % 4]
+                    remote(group, group, along_send.at[s, f, d], along_recv.at[s, f, d], sibling).wait_recv()
+                    relay(s, f, u, u_next, clear, d)
+
+    def last_arrivals():
+        for s, k, f in pairs:
+            u, u_root, w_root, u_next, w_next, du, dw, clear = p_role(k, f)
+
+            @pl.when((du != 0) | (dw != 0))
+            def _():
+                for d in range(2):
+                    group = p_buf.at[s, f * 4 + (u + 2) % 4, :, parts[d]]
+                    remote(group, group, relay_send.at[s, f, d], relay_recv.at[s, f, d], sibling).wait_recv()
+
+        pltpu.make_async_copy(p_buf, p_out, out_sem.at[1]).start()
+
+    @pl.loop(0, chunks + 3 * A_LAG + 2)
     def _(t):
+        for s, k in enumerate(panels):
+            for way in range(2):
+                a_stream(s, k, way, t)
+        for when, act in zip(P_TIMES, (first_arrivals, second_arrivals, third_arrivals, fourth_arrivals, last_arrivals)):
+            pl.when(t == when)(act)
+
+    for s, k in enumerate(panels):
         for way in range(2):
-            for s, k in enumerate(panels):
-                a_stream(s, k, way, t)
-        for quarter in range(4):
-            for s, k in enumerate(panels):
-                p_stream(s, k, quarter, t)
-
-    for s, k in enumerate(panels):
-        x_root, core_root = (k // 2) // 2, (k // 2) % 2
-        for way in range(2):
-            ahead = (x - x_root + 4) % 4 if way == 0 else (x_root - x + 4) % 4
+            ahead, origin, onward, sideways, lag = a_role(k, way)
             half = a_buf.at[s, pl.ds(way * (A_GROUPS // 2), A_GROUPS // 2)]
 
-            @pl.when((core == core_root) & (ahead < 3))
+            @pl.when(onward)
             def _():
                 remote(half, half, a_fwd.at[s, way], a_recv.at[s, 0], sibling).wait_send()
 
-            @pl.when(core == core_root)
+            @pl.when(sideways)
             def _():
                 remote(half, half, a_sib.at[s, way], a_recv.at[s, 0], sibling).wait_send()
 
-        for quarter in range(4):
-            back = quarter % 2
-            first, second = ((y, k // 4), (z, k % 4)) if quarter < 2 else ((z, k % 4), (y, k // 4))
-            e1 = (first[0] - first[1] + 4) % 4 if back == 0 else (first[1] - first[0] + 4) % 4
-            e2 = (second[0] - second[1] + 4) % 4 if back == 0 else (second[1] - second[0] + 4) % 4
-            part = p_buf.at[s, pl.ds(quarter * 2, 2)]
-
-            @pl.when((e2 == 0) & (e1 < 3))
-            def _():
-                remote(part, part, p_trunk.at[s, quarter], p_recv.at[s, 0], sibling).wait_send()
-
-            @pl.when(e2 < 3)
-            def _():
-                remote(part, part, p_branch.at[s, quarter], p_recv.at[s, 0], sibling).wait_send()
+    for s, k, f in pairs:
+        u, u_root, w_root, u_next, w_next, du, dw, clear = p_role(k, f)
+        group = p_buf.at[s, f * 4 + u]
+        half = p_buf.at[s, f * 4 + u, :, parts[0]]
+
+        @pl.when((du == 0) & (dw == 0))
+        def _():
+            for j in range(3):
+                remote(group, group, line_send.at[s, f, j], line_recv.at[s, f], sibling).wait_send()
+
+        for d in range(2):
+            @pl.when(dw == 0)
+            def _():
+                remote(group, group, across_send.at[s, f, d], across_recv.at[s, f, d], sibling).wait_send()
+
+            @pl.when(dw == (1 if d == 0 else 3))
+            def _():
+                remote(half, half, far_send.at[s, f, d], far_recv.at[s, f, d], sibling).wait_send()
+
+            @pl.when(clear[d])
+            def _():
+                remote(group, group, along_send.at[s, f, d], along_recv.at[s, f, d], sibling).wait_send()
+                remote(half, half, relay_send.at[s, f, d], relay_recv.at[s, f, d], sibling).wait_send()
 
     pltpu.make_async_copy(a_buf, a_out, out_sem.at[0]).wait()
     pltpu.make_async_copy(p_buf, p_out, out_sem.at[1]).wait()
@@ -184,6 +271,8 @@
     anywhere = pl.BlockSpec(memory_space=pl.ANY)
     a_shape = (SECTIONS, A_GROUPS, 16, B * B)
     p_shape = (SECTIONS, P_GROUPS, 16, B * B)
+    dma = pltpu.SemaphoreType.DMA
+    ends = [dma((SECTIONS, 2, 2)), dma((SECTIONS, 2, 2))]
     return pl.pallas_call(
         functools.partial(gather_kernel, panel),
         out_shape=(jax.ShapeDtypeStruct(a_shape, jnp.bfloat16), jax.ShapeDtypeStruct(p_shape, jnp.bfloat16)),
@@ -192,15 +281,14 @@
         scratch_shapes=[
             pltpu.VMEM(a_shape, jnp.bfloat16),
             pltpu.VMEM(p_shape, jnp.bfloat16),
-            pltpu.SemaphoreType.DMA((SECTIONS, A_GROUPS * A_CUT)),
-            pltpu.SemaphoreType.DMA((SECTIONS, P_GROUPS * P_CUT)),
-            pltpu.SemaphoreType.DMA((SECTIONS, 2)),
-            pltpu.SemaphoreType.DMA((SECTIONS, 2)),
-            pltpu.SemaphoreType.DMA((SECTIONS, 4)),
-            pltpu.SemaphoreType.DMA((SECTIONS, 4)),
-            pltpu.SemaphoreType.DMA((2, SECTIONS)),
-            pltpu.SemaphoreType.DMA((2,)),
-        ],
+            dma((SECTIONS, A_GROUPS * A_CUT)),
+            dma((SECTIONS, 2)),
+            dma((SECTIONS, 2)),
+            dma((SECTIONS, 2, 3)),
+            dma((SECTIONS, 2)),
+        ]
+        + ends * 4
+        + [dma((2, SECTIONS)), dma((2,))],
         compiler_params=pltpu.CompilerParams(collective_id=1 + panel, has_side_effects=True),
         name=f"gather_{panel}",
     )(a_blocks.reshape(2, A_GROUPS, 16, B * B), p_blocks.reshape(1, P_GROUPS, 16, B * B))
@@ -374,8 +462,8 @@
     return jnp.dot(a, b, preferred_element_type=jnp.float32)
 
 
-UN_Q = 2
-UN_I = 4
+UN_Q = 4
+UN_I = 8
 
 
 def local_kernel(sched, fine_agg, coarse_place, a_ref, p_ref, a_row, a_col, p_row, p_col, q_ref, cols_ref, out_ref,
@@ -394,8 +482,13 @@
         a_par.append(parity(a_col[pick, :]))
         p_par.append(parity(p_col[pick, :]))
 
-    block_of = lax.broadcasted_iota(jnp.int32, (FR, CB * B), 1) // B
-    picked = cols_ref[pl.ds(pl.multiple_of(own_row * FR, FR), FR), :]
+    block_of = (lax.broadcasted_iota(jnp.int32, (FR, CB * B), 1) // B).astype(jnp.float32)
+    groups = cols_ref.shape[1]
+    own = lax.broadcasted_iota(jnp.int32, (FR, groups), 1) == lax.broadcasted_iota(jnp.int32, (FR, groups), 0) + own_row * FR
+    chosen = jnp.where(own, 1.0, 0.0).astype(jnp.bfloat16)
+    picked = lax.dot_general(
+        chosen, cols_ref[...].astype(jnp.float32).astype(jnp.bfloat16), (((1,), (1,)), ((), ())), preferred_element_type=jnp.float32
+    )
     hit = block_of == picked[:, 0:1]
     for n in range(1, picked.shape[1]):
         hit = hit | (block_of == picked[:, n:n + 1])
@@ -448,6 +541,13 @@
         @pl.loop(0, FR, step=UN_I)
         def _(first):
             terms = []
+            turned = []
+            for t in range(4):
+                groups = []
+                for high in range(B // 8):
+                    rows = [product[t, pl.ds(pl.multiple_of((high * 8 + low) * FR + first, 8), 8), :] for low in range(8)]
+                    groups.append(jnp.swapaxes(jnp.stack(rows, axis=0), 0, 1))
+                turned.append(groups)
             for u in range(UN_I):
                 i = first + u
                 pair = q_rows[pl.ds(i, B // 2, stride=FR), :]
@@ -456,7 +556,7 @@
                 for j in range(0, 4, 2):
                     tops, bottoms = [], []
                     for t in (j, j + 1):
-                        block = product[t, pl.ds(i, B, stride=FR), :]
+                        block = jnp.concatenate([group[u] for group in turned[t]], axis=0)
                         top = block.astype(jnp.bfloat16)
                         tops.append(top)
                         bottoms.append((block - top.astype(jnp.float32)).astype(jnp.bfloat16))
@@ -508,7 +608,7 @@
 
 
 def per_device(a_blocks, a_row, a_col, p_blocks, p_row, p_col, q_blocks, sched, fine_agg, coarse_place, prod_cols):
-    other = sched[0] + sched[1] - LAST
+    other = jnp.sum(sched) - LAST
     a, p = lax.switch(other, [functools.partial(gather_panels, k) for k in range(LAST)], a_blocks, p_blocks)
     term = local_terms(
         sched,
@@ -521,7 +621,7 @@
         p_row,
         p_col,
         q_blocks,
-        prod_cols,
+        prod_cols.T,
     )
     return reduce_terms(term.reshape(2, 4, 4, 4, B, HALF))
 

time: 149 us -> 130 us (0.87)
  Pallas kernels: 143 us -> 125 us
  local copies, waits for them, and re-layouts: 5.17 us -> 2.31 us
    pallas_call x1, Pallas kernels: 53.6 us -> 41.2 us  [gather_panels(): pl.pallas_call(functools.partial(gather_kernel, panel), out_shape=(jax.Sh...]
    pallas_call x1, Pallas kernels: 39.3 us -> 32.2 us  [local_terms(): pl.pallas_call(local_kernel, out_shape=jax.ShapeDtypeStruct((2, 64, B, HA...]
    unnamed x2 -> x1, local copies, waits for them, and re-layouts: 3.86 us -> 2.31 us
where the time goes in v4:
time: 130 us; the launch traced here: 129 us
  Pallas kernels  125 us (96%)
  local copies, waits for them, and re-layouts  2.31 us (2%)
    pallas_call x1, Pallas kernels, reduce_terms(): pl.pallas_call(reduce_kernel, out_shape=jax.ShapeDtypeStruct((PART, 2 * H...  51.4 us
    pallas_call x1, Pallas kernels, gather_panels(): pl.pallas_call(functools.partial(gather_kernel, panel), out_shape=(jax.Sh...  41.2 us
    pallas_call x1, Pallas kernels, local_terms(): pl.pallas_call(local_kernel, out_shape=jax.ShapeDtypeStruct((2, 64, B, HA...  32.2 us

profile of v4, /device:TPU:6, one launch (start us, length us, event | category | flops | bytes accessed | tf_op | source)
XLA Modules:
  0.0 129.4 jit_solution(5974725121317202163)
XLA Ops:
  0.0 1.3 reduce_sum.9
  1.9 41.5 %conditional.1 = (bf16[2,256,4096]{2,1,0:T(8,128)(2,1)}, bf16[2,128,4096]{2,1,0:T(8,128)(2,1)S(1)}) conditional(s32[]{:T(128)} %clamp.3, (bf16[2,256,4096]{2,1,0:T(8,128)(2,1)}, bf16[1,128,4096]{2,1,0:T(8,128)(2,1)}) %tuple.95, (bf16[2,256,4096]{2,1,0:T(8,128)(2,1)}, bf16[1,128,4096]{2,1,0:T(8,128)(2,1)}) %tuple.95, ...), branch_computations={%region_1.0_spmd, %region_2.0_spmd, %region_3.0_spmd, %region_4.0_... | conditional | bytes 16 | solution.py:612
  2.0 41.2 %gather_2.1 = (bf16[2,16,16,4096]{3,2,1,0:T(8,128)(2,1)}, bf16[2,8,16,4096]{3,2,1,0:T(8,128)(2,1)S(1)}) custom-call(bf16[2,16,16,4096]{3,2,1,0:T(8,128)(2,1)} %bitcast.64, bf16[1,8,16,4096]{3,2,1,0:T(8,128)(2,1)} %bitcast.79), custom_call_target="tpu_custom_call" | custom-call | tf_op jit(solution)/shard_map/cond/branch_2_fun/gather_2/pallas_call | solution.py:276
  43.5 32.2 %local_terms.1 = bf16[2,64,64,512]{3,2,1,0:T(8,128)(2,1)} custom-call(s32[2]{0:T(128)} %sched.1, s32[512]{0:T(512)} %fine_agg.1, s32[64]{0:T(128)} %coarse_place.1, bf16[2,256,4096]{2,1,0:T(8,128)(2,1)} %get-tuple-element.159.a_ref, bf16[2,128,4096]{2,1,0:T(8,128)(2,1)S(1)} %get-tuple-element.160.p_ref, s32[16,256]{1,0:T(8,128)} %a_row.1, s32[16,256]{1,0:T(8,128)} %a_col.1, ...), custom_call_target="tpu_custom_call" | custom-call | tf_op jit(solution)/shard_map/local_terms/pallas_call | solution.py:589
  75.6 51.4 %reduce_terms.1 = f32[256,1024]{1,0:T(8,128)} custom-call(bf16[2,4,4,4,64,512]{5,4,3,2,1,0:T(8,128)(2,1)} %bitcast.92), custom_call_target="tpu_custom_call" | custom-call | tf_op jit(solution)/shard_map/reduce_terms/pallas_call | solution.py:415
  127.1 2.3 %copy.43 = f32[256,1024]{1,0:T(8,128)} copy(f32[256,1024]{1,0:T(8,128)} %reduce_terms.1) | data formatting | bytes 2097152

commit v5 on v4

--- a/solution.py
+++ b/solution.py
@@ -289,7 +289,7 @@
         ]
         + ends * 4
         + [dma((2, SECTIONS)), dma((2,))],
-        compiler_params=pltpu.CompilerParams(collective_id=1 + panel, has_side_effects=True),
+        compiler_params=pltpu.CompilerParams(collective_id=1 + panel, has_side_effects=True, vmem_limit_bytes=16 * 1024 * 1024),
         name=f"gather_{panel}",
     )(a_blocks.reshape(2, A_GROUPS, 16, B * B), p_blocks.reshape(1, P_GROUPS, 16, B * B))
 
@@ -431,7 +431,7 @@
             pltpu.SemaphoreType.DMA((2, 2, 3)),
             pltpu.SemaphoreType.DMA((2, 2, 3)),
         ],
-        compiler_params=pltpu.CompilerParams(collective_id=0, has_side_effects=True, vmem_limit_bytes=62 * 1024 * 1024),
+        compiler_params=pltpu.CompilerParams(collective_id=0, has_side_effects=True, vmem_limit_bytes=16 * 1024 * 1024),
         name="reduce_terms",
     )(term)
 
@@ -467,7 +467,7 @@
 
 
 def local_kernel(sched, fine_agg, coarse_place, a_ref, p_ref, a_row, a_col, p_row, p_col, q_ref, cols_ref, out_ref,
-                 a_dense, p_rows, p_dense, product, total, staged, mask, q_rows, out_sem):
+                 a_dense, p_rows, p_dense, product, total, mask, q_rows):
     own_row = lax.axis_index("row")
     row_index = lax.broadcasted_iota(jnp.int32, (256, 256), 0)
     col_index = lax.broadcasted_iota(jnp.int32, (256, 256), 1)
@@ -575,12 +575,7 @@
 
         @pl.loop(0, 64)
         def _(g):
-            staged[h, g] = total[g].astype(jnp.bfloat16)
-
-        pltpu.make_async_copy(staged.at[h], out_ref.at[h], out_sem.at[h]).start()
-
-    for h in range(2):
-        pltpu.make_async_copy(staged.at[h], out_ref.at[h], out_sem.at[h]).wait()
+            out_ref[h, g] = total[g].astype(jnp.bfloat16)
 
 
 def local_terms(sched, fine_agg, coarse_place, a, p, a_row, a_col, p_row, p_col, q, prod_cols):
@@ -590,19 +585,17 @@
         local_kernel,
         out_shape=jax.ShapeDtypeStruct((2, 64, B, HALF), jnp.bfloat16),
         in_specs=[smem] * 3 + [vmem] * 8,
-        out_specs=pl.BlockSpec(memory_space=pl.ANY),
+        out_specs=vmem,
         scratch_shapes=[
             pltpu.VMEM((FR * B, SECTIONS * KB * B), jnp.bfloat16),
             pltpu.VMEM((SECTIONS, KB * B, CB * B), jnp.bfloat16),
             pltpu.VMEM((SECTIONS * KB * B, CB * B), jnp.bfloat16),
             pltpu.VMEM((4, FR * B, LANES), jnp.float32),
             pltpu.VMEM((64, B, HALF), jnp.float32),
-            pltpu.VMEM((2, 64, B, HALF), jnp.bfloat16),
             pltpu.VMEM((FR, CB * B), jnp.float32),
             pltpu.VMEM((FR * B // 2, LANES), jnp.float32),
-            pltpu.SemaphoreType.DMA((2,)),
         ],
-        compiler_params=pltpu.CompilerParams(vmem_limit_bytes=60 * 1024 * 1024),
+        compiler_params=pltpu.CompilerParams(vmem_limit_bytes=44 * 1024 * 1024),
         name="local_terms",
     )(sched, fine_agg, coarse_place, a, p, a_row, a_col, p_row, p_col, q, prod_cols)
 

time: 130 us -> 126 us (0.969)
  Pallas kernels: 125 us -> 123 us
    pallas_call x1, Pallas kernels: 51.4 us -> 54.2 us  [reduce_terms(): pl.pallas_call(reduce_kernel, out_shape=jax.ShapeDtypeStruct((PART, 2 * H...]
    pallas_call x1, Pallas kernels: 41.2 us -> 38.7 us  [gather_panels(): pl.pallas_call(functools.partial(gather_kernel, panel), out_shape=(jax.Sh...]
    pallas_call x1, Pallas kernels: 32.2 us -> 30.3 us  [local_terms(): pl.pallas_call(local_kernel, out_shape=jax.ShapeDtypeStruct((2, 64, B, HA...]
where the time goes in v5:
time: 126 us
  Pallas kernels  123 us (98%)
  other arithmetic  1.29 us (1%)
    pallas_call x1, Pallas kernels, reduce_terms(): pl.pallas_call(reduce_kernel, out_shape=jax.ShapeDtypeStruct((PART, 2 * H...  54.2 us
    pallas_call x1, Pallas kernels, gather_panels(): pl.pallas_call(functools.partial(gather_kernel, panel), out_shape=(jax.Sh...  38.7 us
    pallas_call x1, Pallas kernels, local_terms(): pl.pallas_call(local_kernel, out_shape=jax.ShapeDtypeStruct((2, 64, B, HA...  30.3 us

profile of v5, /device:TPU:6, one launch (start us, length us, event | category | flops | bytes accessed | tf_op | source)
XLA Modules:
  0.0 126.5 jit_solution(14261468097454133949)
XLA Ops:
  0.0 1.3 %reduce_sum.9 = s32[]{:T(128)} reduce(s32[2]{0:T(128)} %sched.1, s32[]{:T(128)} %constant.1.clone.1), dimensions={0}, to_apply=%region_0.0 | reduce | flops 1 | bytes 16 | tf_op jit(solution)/shard_map/reduce_sum | solution.py:604
  1.9 0.0 copy-start
  2.0 0.0 copy-start.1
  2.0 0.0 copy-start.2
  2.0 0.0 copy-start.3
  2.0 0.0 copy-start.4
  2.0 0.0 copy-start.5
  2.0 0.0 copy-start.6
  2.0 0.0 copy-start.7
  2.0 0.0 copy-start.8
  2.1 38.9 %conditional.1 = (bf16[2,256,4096]{2,1,0:T(8,128)(2,1)}, bf16[2,128,4096]{2,1,0:T(8,128)(2,1)S(1)}) conditional(s32[]{:T(128)} %clamp.3, (bf16[2,256,4096]{2,1,0:T(8,128)(2,1)}, bf16[1,128,4096]{2,1,0:T(8,128)(2,1)}) %tuple.95, (bf16[2,256,4096]{2,1,0:T(8,128)(2,1)}, bf16[1,128,4096]{2,1,0:T(8,128)(2,1)}) %tuple.95, ...), branch_computations={%region_1.0_spmd, %region_2.0_spmd, %region_3.0_spmd, %region_4.0_... | conditional | bytes 16 | solution.py:605
  2.1 38.7 %gather_3.1 = (bf16[2,16,16,4096]{3,2,1,0:T(8,128)(2,1)}, bf16[2,8,16,4096]{3,2,1,0:T(8,128)(2,1)S(1)}) custom-call(bf16[2,16,16,4096]{3,2,1,0:T(8,128)(2,1)} %bitcast.67, bf16[1,8,16,4096]{3,2,1,0:T(8,128)(2,1)} %bitcast.82), custom_call_target="tpu_custom_call" | custom-call | tf_op jit(solution)/shard_map/cond/branch_3_fun/gather_3/pallas_call | solution.py:276
  41.0 0.0 copy-done
  41.0 0.0 copy-done.1
  41.0 0.0 copy-done.2
  41.0 0.0 copy-done.3
  41.0 0.0 copy-done.4
  41.0 0.0 copy-done.5
  41.1 0.0 copy-done.6
  41.1 0.0 copy-done.7
  41.1 0.0 copy-done.8
  41.1 30.3 %local_terms.1 = bf16[2,64,64,512]{3,2,1,0:T(8,128)(2,1)S(1)} custom-call(s32[2]{0:T(128)S(1)} %copy-done.7, s32[512]{0:T(512)S(1)} %copy-done.6, s32[64]{0:T(128)S(1)} %copy-done.8, bf16[2,256,4096]{2,1,0:T(8,128)(2,1)} %get-tuple-element.159.a_ref, bf16[2,128,4096]{2,1,0:T(8,128)(2,1)S(1)} %get-tuple-element.160.p_ref, s32[16,256]{1,0:T(8,128)S(1)} %copy-done.1, ...), custom_call_target="tpu_custom_call" | custom-call | tf_op jit(solution)/shard_map/local_terms/pallas_call | solution.py:584
  71.4 54.2 %reduce_terms.1 = f32[256,1024]{1,0:T(8,128)S(1)} custom-call(bf16[2,4,4,4,64,512]{5,4,3,2,1,0:T(8,128)(2,1)S(1)} %bitcast.62), custom_call_target="tpu_custom_call" | custom-call | tf_op jit(solution)/shard_map/reduce_terms/pallas_call | solution.py:415
  125.5 1.0 copy.43
Async XLA Ops:
  1.9 39.0 %copy-start = (bf16[32,4096]{1,0:T(8,128)(2,1)S(1)}, bf16[32,4096]{1,0:T(8,128)(2,1)}, u32[]{:S(2)}) copy-start(bf16[32,4096]{1,0:T(8,128)(2,1)} %q_ref.1) | copy-start | bytes 786436
  2.0 39.0 %copy-start.1 = (s32[16,256]{1,0:T(8,128)S(1)}, s32[16,256]{1,0:T(8,128)}, u32[]{:S(2)}) copy-start(s32[16,256]{1,0:T(8,128)} %a_row.1) | copy-start | bytes 49156
  2.0 39.0 %copy-start.2 = (s32[16,256]{1,0:T(8,128)S(1)}, s32[16,256]{1,0:T(8,128)}, u32[]{:S(2)}) copy-start(s32[16,256]{1,0:T(8,128)} %a_col.1) | copy-start | bytes 49156
  2.0 39.0 %copy-start.3 = (s32[512,8]{0,1:T(8,128)S(1)}, s32[512,8]{0,1:T(8,128)}, u32[]{:S(2)}) copy-start(s32[512,8]{0,1:T(8,128)} %param.36) | copy-start | bytes 49156
  2.0 39.0 %copy-start.4 = (s32[16,128]{1,0:T(8,128)S(1)}, s32[16,128]{1,0:T(8,128)}, u32[]{:S(2)}) copy-start(s32[16,128]{1,0:T(8,128)} %p_row.1) | copy-start | bytes 24580
  2.0 39.0 %copy-start.5 = (s32[16,128]{1,0:T(8,128)S(1)}, s32[16,128]{1,0:T(8,128)}, u32[]{:S(2)}) copy-start(s32[16,128]{1,0:T(8,128)} %p_col.1) | copy-start | bytes 24580
  2.0 39.0 %copy-start.6 = (s32[512]{0:T(512)S(1)}, s32[512]{0:T(512)}, u32[]{:S(2)}) copy-start(s32[512]{0:T(512)} %fine_agg.1) | copy-start | bytes 6148
  2.0 39.0 %copy-start.7 = (s32[2]{0:T(128)S(1)}, s32[2]{0:T(128)}, u32[]{:S(2)}) copy-start(s32[2]{0:T(128)} %sched.1) | copy-start | bytes 28
  2.0 39.0 %copy-start.8 = (s32[64]{0:T(128)S(1)}, s32[64]{0:T(128)}, u32[]{:S(2)}) copy-start(s32[64]{0:T(128)} %coarse_place.1) | copy-start | bytes 772

commit v6 on v5

--- a/solution.py
+++ b/solution.py
@@ -22,7 +22,7 @@
 P_GROUPS = 8
 A_CUT = 1
 A_LAG = 2
-P_TIMES = (5, 7, 8, 10, 13)
+P_TIMES = (4, 7, 9, 12, 15)
 
 
 def remote(src, dst, send_sem, recv_sem, target):

time: 126 us -> 123 us (0.976); the launches traced: 126 us -> 121 us
  Pallas kernels: 123 us -> 117 us
    pallas_call x1, Pallas kernels: 54.2 us -> 51.1 us  [reduce_terms(): pl.pallas_call(reduce_kernel, out_shape=jax.ShapeDtypeStruct((PART, 2 * H...]
    pallas_call x1, Pallas kernels: 38.7 us -> 35.7 us  [gather_panels(): pl.pallas_call(functools.partial(gather_kernel, panel), out_shape=(jax.Sh...]
where the time goes in v6:
time: 123 us; the launch traced here: 121 us
  Pallas kernels  117 us (95%)
  other arithmetic  1.29 us (1%)
    pallas_call x1, Pallas kernels, reduce_terms(): pl.pallas_call(reduce_kernel, out_shape=jax.ShapeDtypeStruct((PART, 2 * H...  51.1 us
    pallas_call x1, Pallas kernels, gather_panels(): pl.pallas_call(functools.partial(gather_kernel, panel), out_shape=(jax.Sh...  35.7 us
    pallas_call x1, Pallas kernels, local_terms(): pl.pallas_call(local_kernel, out_shape=jax.ShapeDtypeStruct((2, 64, B, HA...  30.3 us

profile of v6, /device:TPU:6, one launch (start us, length us, event | category | flops | bytes accessed | tf_op | source)
XLA Modules:
  0.0 120.6 jit_solution(583042190541102574)
XLA Ops:
  0.0 1.3 %reduce_sum.9 = s32[]{:T(128)} reduce(s32[2]{0:T(128)} %sched.1, s32[]{:T(128)} %constant.1.clone.1), dimensions={0}, to_apply=%region_0.0 | reduce | flops 1 | bytes 16 | tf_op jit(solution)/shard_map/reduce_sum | solution.py:604
  1.9 0.0 copy-start
  2.0 0.0 copy-start.1
  2.0 0.0 copy-start.2
  2.0 0.0 copy-start.3
  2.0 0.0 copy-start.4
  2.0 0.0 copy-start.5
  2.0 0.0 copy-start.6
  2.0 0.0 copy-start.7
  2.0 0.0 copy-start.8
  2.1 36.0 %conditional.1 = (bf16[2,256,4096]{2,1,0:T(8,128)(2,1)}, bf16[2,128,4096]{2,1,0:T(8,128)(2,1)S(1)}) conditional(s32[]{:T(128)} %clamp.3, (bf16[2,256,4096]{2,1,0:T(8,128)(2,1)}, bf16[1,128,4096]{2,1,0:T(8,128)(2,1)}) %tuple.95, (bf16[2,256,4096]{2,1,0:T(8,128)(2,1)}, bf16[1,128,4096]{2,1,0:T(8,128)(2,1)}) %tuple.95, ...), branch_computations={%region_1.0_spmd, %region_2.0_spmd, %region_3.0_spmd, %region_4.0_... | conditional | bytes 16 | solution.py:605
  2.1 35.7 %gather_4.1 = (bf16[2,16,16,4096]{3,2,1,0:T(8,128)(2,1)}, bf16[2,8,16,4096]{3,2,1,0:T(8,128)(2,1)S(1)}) custom-call(bf16[2,16,16,4096]{3,2,1,0:T(8,128)(2,1)} %bitcast.68, bf16[1,8,16,4096]{3,2,1,0:T(8,128)(2,1)} %bitcast.83), custom_call_target="tpu_custom_call" | custom-call | tf_op jit(solution)/shard_map/cond/branch_4_fun/gather_4/pallas_call | solution.py:276
  38.1 0.0 copy-done
  38.1 0.0 copy-done.1
  38.1 0.0 copy-done.2
  38.1 0.0 copy-done.3
  38.1 0.0 copy-done.4
  38.1 0.0 copy-done.5
  38.1 0.0 copy-done.6
  38.2 0.0 copy-done.7
  38.2 0.0 copy-done.8
  38.2 30.3 %local_terms.1 = bf16[2,64,64,512]{3,2,1,0:T(8,128)(2,1)S(1)} custom-call(s32[2]{0:T(128)S(1)} %copy-done.7, s32[512]{0:T(512)S(1)} %copy-done.6, s32[64]{0:T(128)S(1)} %copy-done.8, bf16[2,256,4096]{2,1,0:T(8,128)(2,1)} %get-tuple-element.159.a_ref, bf16[2,128,4096]{2,1,0:T(8,128)(2,1)S(1)} %get-tuple-element.160.p_ref, s32[16,256]{1,0:T(8,128)S(1)} %copy-done.1, ...), custom_call_target="tpu_custom_call" | custom-call | tf_op jit(solution)/shard_map/local_terms/pallas_call | solution.py:584
  68.4 51.1 %reduce_terms.1 = f32[256,1024]{1,0:T(8,128)S(1)} custom-call(bf16[2,4,4,4,64,512]{5,4,3,2,1,0:T(8,128)(2,1)S(1)} %bitcast.62), custom_call_target="tpu_custom_call" | custom-call | tf_op jit(solution)/shard_map/reduce_terms/pallas_call | solution.py:415
  119.6 1.0 copy.43
Async XLA Ops:
  1.9 36.1 %copy-start = (bf16[32,4096]{1,0:T(8,128)(2,1)S(1)}, bf16[32,4096]{1,0:T(8,128)(2,1)}, u32[]{:S(2)}) copy-start(bf16[32,4096]{1,0:T(8,128)(2,1)} %q_ref.1) | copy-start | bytes 786436
  2.0 36.1 %copy-start.1 = (s32[16,256]{1,0:T(8,128)S(1)}, s32[16,256]{1,0:T(8,128)}, u32[]{:S(2)}) copy-start(s32[16,256]{1,0:T(8,128)} %a_row.1) | copy-start | bytes 49156
  2.0 36.1 %copy-start.2 = (s32[16,256]{1,0:T(8,128)S(1)}, s32[16,256]{1,0:T(8,128)}, u32[]{:S(2)}) copy-start(s32[16,256]{1,0:T(8,128)} %a_col.1) | copy-start | bytes 49156
  2.0 36.1 %copy-start.3 = (s32[512,8]{0,1:T(8,128)S(1)}, s32[512,8]{0,1:T(8,128)}, u32[]{:S(2)}) copy-start(s32[512,8]{0,1:T(8,128)} %param.36) | copy-start | bytes 49156
  2.0 36.1 %copy-start.4 = (s32[16,128]{1,0:T(8,128)S(1)}, s32[16,128]{1,0:T(8,128)}, u32[]{:S(2)}) copy-start(s32[16,128]{1,0:T(8,128)} %p_row.1) | copy-start | bytes 24580
  2.0 36.1 %copy-start.5 = (s32[16,128]{1,0:T(8,128)S(1)}, s32[16,128]{1,0:T(8,128)}, u32[]{:S(2)}) copy-start(s32[16,128]{1,0:T(8,128)} %p_col.1) | copy-start | bytes 24580
  2.0 36.1 %copy-start.6 = (s32[512]{0:T(512)S(1)}, s32[512]{0:T(512)}, u32[]{:S(2)}) copy-start(s32[512]{0:T(512)} %fine_agg.1) | copy-start | bytes 6148
  2.0 36.1 %copy-start.7 = (s32[2]{0:T(128)S(1)}, s32[2]{0:T(128)}, u32[]{:S(2)}) copy-start(s32[2]{0:T(128)} %sched.1) | copy-start | bytes 28
  2.0 36.1 %copy-start.8 = (s32[64]{0:T(128)S(1)}, s32[64]{0:T(128)}, u32[]{:S(2)}) copy-start(s32[64]{0:T(128)} %coarse_place.1) | copy-start | bytes 772
